TPU v7x, 128 devices: a whole 4x4x4 slice. The times are simulated.
128 devices in a mesh: win: 16 (over y, x_hi, core), tile: 8 (over x_lo, z).
Axes of the slice: x: 4 (x_hi: 2, x_lo: 2; x = x_hi * 2 + x_lo), y: 4, z: 4, core: 2. Of those that a mesh axis runs over, the one named last changes fastest.
Arguments:
- flux: bfloat16 [3840, 65536], P('win', 'tile'), may hold values from -6 to 6
- prior_std: float32 [3840, 65536], P('win', 'tile'), may hold values from 0.3 to 3
- footprint: bfloat16 [16384, 128, 128], P('win', 'tile'), may hold values from 0.0099487305 to 1
- obs_value: float32 [16384], P('win'), may hold values from -180 to 180
- obs_weight: float32 [16384], P('win'), may hold values from 0.002 to 0.02
- obs_hour: int32 [16384], P('win'), may hold values from 0 to 239
- hour_offset: int32 [16384, 128], P('win', 'tile'), may hold values from 0 to 239
- block_cell: int32 [16384, 128], P('win', 'tile'), may hold values from 0 to 63
Outputs:
- gradient: float32 [3840, 65536], P('win', 'tile')
Inputs may be any that keep to these rules, and one draw needn't show every extreme that they name: `block_cell`: index of a block of 128 cells within the tile.
All inputs are finite; a program needn't handle non-finite values.
Results may differ from a plain program's by a relative error of at most 0.0003.
Values may be sent and summed in bfloat16 or wider, within the bound.
A program may use at most 128 MiB of HBM per device.

v0:
```python
import functools

import jax
import jax.numpy as jnp
import numpy as np
from jax import lax
from jax.experimental import pallas as pl
from jax.experimental.pallas import tpu as pltpu
from jax.sharding import PartitionSpec as P


KH = 24
LANES = 128
CELLS = 64
NBIN = 2 * CELLS
HEAD = 41 * LANES
NEAR = 32
META = CELLS + CELLS + 8
F32, BF16, I32 = jnp.float32, jnp.bfloat16, jnp.int32
NT = (((1,), (1,)), ((), ()))
MESH = pl.DeviceIdType.MESH
VM = pl.BlockSpec(memory_space=pltpu.VMEM)
HBM = pl.BlockSpec(memory_space=pltpu.HBM)


def tab_of(half):
    return pl.BlockSpec((8, LANES), lambda *_: (META // 8 * (half + 1) - 1, 0), memory_space=pltpu.SMEM)


def tabv_of(half):
    return pl.BlockSpec((8, LANES), lambda *_: (META // 8 * (half + 1) - 1, 0))


def tabs_from(metas):
    return [metas[0], metas[0], metas[1], metas[1]]


def iota(shape, dim):
    return lax.broadcasted_iota(I32, shape, dim)


def dot(a, b):
    return jnp.dot(a, b, preferred_element_type=F32)


def halves(v):
    top = v.astype(BF16).astype(F32)
    return top, v - top


def pick(table, lane):
    return jnp.take_along_axis(table, jnp.broadcast_to(lane, table.shape), axis=1, mode="promise_in_bounds")


def from_behind(value, axis, steps):
    count = lax.axis_size(axis)
    initial, last = (max(0, -steps), min(count, count - steps))
    return lax.ppermute(value, axis, [(source, source + steps) for source in range(initial, last)])


def extended(cells, sides, width):
    for axis, dim in sides:
        count = lax.axis_size(axis)
        ends = count - 1
        head = lax.slice_in_dim(cells, 0, width, axis=dim)
        tail = lax.slice_in_dim(cells, cells.shape[dim] - width, cells.shape[dim], axis=dim)
        cells = jnp.concatenate(
            [
                lax.ppermute(tail, axis, [(i, (i + 1) % count) for i in range(ends)]),
                cells,
                lax.ppermute(head, axis, [((i + 1) % count, i) for i in range(ends)]),
            ],
            axis=dim,
        )
    return cells


def misfits(partial_value, obs_value, obs_weight):
    predicted = lax.psum(partial_value, "tile")
    return (predicted - obs_value) * obs_weight


def general(flux, prior_std, footprint, obs_value, obs_weight, obs_hour, hour_offset, block_cell):
    hours = flux.shape[0]
    cells = flux.shape[1]
    width = footprint.shape[2]
    per_hour = cells // width
    earlier = from_behind(flux, "win", 1)
    joined = jnp.concatenate([earlier, flux], axis=0).reshape(2 * hours * per_hour, width)
    flat = (hours + obs_hour[:, None] - hour_offset) * per_hour + block_cell
    picked = joined[flat]
    partial_value = jnp.einsum("onc,onc->o", footprint, picked, preferred_element_type=jnp.float32)
    weighted = misfits(partial_value, obs_value, obs_weight)
    contrib = weighted[:, None, None] * footprint.astype(jnp.float32)
    summed = jax.ops.segment_sum(
        contrib.reshape(-1, width), flat.reshape(-1), num_segments=2 * hours * per_hour
    )
    summed = summed.reshape(2 * hours, cells)
    returned = from_behind(summed[:hours], "win", -1)
    adjoint = summed[hours:] + returned
    scaled = prior_std * adjoint
    rim = extended(scaled, (("win", 0),), KH)
    rows = jnp.arange(hours, dtype=jnp.int32)[:, None]
    columns = jnp.arange(hours + 2 * KH, dtype=jnp.int32)[None, :]
    distance = columns - rows - KH
    kernel = jnp.where(
        jnp.abs(distance) <= KH, jnp.exp(-2.0 * jnp.abs(distance).astype(jnp.float32) / KH), 0.0
    )
    smoothed = jnp.dot(
        kernel, rim, preferred_element_type=jnp.float32, precision=lax.Precision.HIGHEST
    )
    return prior_std * smoothed


class Sorter:
    def __init__(self, nobs, hb, oh_ref, off_ref, cell_ref, metas, keyv, hourv, posv, tabv):
        self.nobs, self.hb, self.inputs, self.metas = nobs, hb, (oh_ref, off_ref, cell_ref), metas
        self.keyv, self.hourv, self.posv, self.tabv = keyv, hourv, posv, tabv
        self.nblk = off_ref.shape[0]
        self.lines = self.nblk * nobs // LANES
        self.cap = capacity(self.nblk * nobs)

    def prepare(self, which, aside):
        nobs, nblk, cap, lines = self.nobs, self.nblk, self.cap, self.lines
        keyv, hourv, posv, metas = self.keyv, self.hourv, self.posv, self.metas
        oh_ref, off_ref, cell_ref = self.inputs
        per = nobs // LANES
        span = HEAD // LANES - 1
        at0 = which * META
        bins = iota((NBIN, LANES), 0)
        lanes = iota((NBIN, LANES), 1)
        upper = (bins < lanes).astype(BF16)
        ones = jnp.ones((LANES, LANES), BF16)
        same = (bins // CELLS) == (lanes // CELLS)
        below = jnp.where(same & (lanes < bins), 1.0, 0.0).astype(BF16)
        before = jnp.where(same & (bins < lanes), 1.0, 0.0).astype(BF16)
        for c in range(per):
            cut = slice(which * nobs + c * LANES, which * nobs + (c + 1) * LANES)
            hour = oh_ref[:, cut] - off_ref[:, cut]
            early = hour < 0
            hour = jnp.where(early, hour + self.hb, hour)
            key = jnp.where(early, cell_ref[:, cut] + CELLS, cell_ref[:, cut])
            rim = (hour < KH) | (hour >= self.hb - KH)
            at = slice(c * nblk, (c + 1) * nblk)
            keyv[0, at, :] = jnp.where(rim, key, -1)
            keyv[1, at, :] = jnp.where(rim, -1, key)
            keyv[2, at, :] = key
            hourv[at, :] = (hour + 1).astype(F32)

        def count(r, total):
            first, second = total
            for u in range(4):
                first = first + jnp.where(bins == keyv[0, pl.ds(r * 4 + u, 1), :], 1.0, 0.0)
                second = second + jnp.where(bins == keyv[1, pl.ds(r * 4 + u, 1), :], 1.0, 0.0)
                aside(0, r, u)
            return first, second

        zero = jnp.zeros((NBIN, LANES), F32)
        first, second = lax.fori_loop(0, lines // 4, count, (zero, zero))
        first, second = first.astype(BF16), second.astype(BF16)
        ahead = [dot(v, upper) for v in (first, second)]
        rim_s = dot(first, ones)
        cnt_s = rim_s + dot(second, ones)
        rim_l = lax.dot_general(ones[:8], first, NT, preferred_element_type=F32)
        cnt_l = rim_l + lax.dot_general(ones[:8], second, NT, preferred_element_type=F32)

        def starts(cnt, left):
            tiles = jnp.floor((cnt + 15.0) * (1.0 / 16.0))
            coarse = jnp.floor(tiles * (1.0 / 128.0))
            fine = tiles - 128.0 * coarse

            def run(v):
                return dot(below, v.astype(BF16)) if left else dot(v.astype(BF16), before)

            return 16.0 * (128.0 * run(coarse) + run(fine))

        tight_l = starts(cnt_l, False)
        base = starts(cnt_s, True) + jnp.where(bins >= CELLS, float(cap), 0.0)
        line8 = iota((8, LANES), 0)
        limit = float(span * LANES)
        far = jnp.where((cnt_l > float(LANES)) | (rim_l > float(NEAR)) | (tight_l + cnt_l > limit), 1.0, 0.0)
        over = jnp.max(far, axis=1, keepdims=True)
        tab = jnp.where(line8 == 0, jnp.minimum(cnt_l, float(LANES)),
                        jnp.where(line8 == 1, jnp.minimum(tight_l, limit), over)).astype(I32)
        self.tabv[...] = tab
        metas[0][at0 + 2 * CELLS:at0 + META, :] = tab
        metas[1][at0 + 2 * CELLS:at0 + META, :] = pltpu.roll(tab, CELLS, 1)
        for turn in range(2):
            def place(r, acc):
                for u in range(4):
                    at = pl.ds(r * 4 + u, 1)
                    hot = bins == keyv[turn, at, :]
                    posf = jnp.sum(jnp.where(hot, acc, 0.0), axis=0, keepdims=True).astype(I32)
                    posv[at, :] = posf if turn == 0 else posv[at, :] + posf
                    acc = jnp.where(hot, acc + 1.0, acc)
                    aside(1 + turn, r, u)
                return acc

            lax.fori_loop(0, lines // 4, place, base + ahead[turn] + (rim_s if turn else 0.0))
        aside(-1, 0, 0)
        starts_l = tight_l + jnp.where(iota((8, LANES), 1) >= CELLS, float(cap), 0.0)
        for g in range(lines // 8):
            at = slice(g * 8, (g + 1) * 8)
            key = keyv[2, at, :]
            rank = posv[at, :] - pick(starts_l, key).astype(I32)
            keyv[0, at, :] = rank
            spot = jnp.where(rank < LANES, (key & (CELLS - 1)) * LANES + rank, -1)
            lo = at0 + CELLS + g * 8
            metas[0][lo:lo + 8, :] = jnp.where(key < CELLS, spot, -1)
            metas[1][lo:lo + 8, :] = jnp.where(key < CELLS, -1, spot)
        obs = iota((1, LANES), 1).astype(F32)
        done = zero
        for c in range(per):
            def gather(r, acc):
                marks, spots = [], []
                for u in range(2):
                    at = pl.ds(c * nblk + r * 2 + u, 1)
                    hot = bins == keyv[2, at, :]
                    marks.append(jnp.concatenate(
                        [jnp.where(hot, v, 0.0).astype(BF16) for v in (hourv[at, :], obs)], axis=0))
                    spots.append(jnp.where(bins == keyv[0, at, :], 1.0, 0.0).astype(BF16))
                    aside(3, r + c * (nblk // 2), u)
                return acc + lax.dot_general(jnp.concatenate(marks, axis=1), jnp.concatenate(spots, axis=1), NT,
                                             preferred_element_type=F32)

            acc = lax.fori_loop(0, nblk // 2, gather, jnp.zeros((2 * NBIN, LANES), F32))
            hour, low = acc[:NBIN], acc[NBIN:]
            done = done + jnp.where(hour > 0.0, hour + 256.0 * (low + float(c * LANES)), 0.0)
        done = done.astype(I32)
        metas[0][at0:at0 + CELLS, :] = done[:CELLS]
        metas[1][at0:at0 + CELLS, :] = done[CELLS:]


def capacity(n):
    return n + CELLS * 16 + LANES


def blank_block(rows, cap, q):
    blocks = HEAD // LANES
    q = jnp.minimum(q, 2 * blocks - 1)
    at = jnp.where(q < blocks, q, q - blocks + cap // LANES)
    rows[pl.ds(pl.multiple_of(at * LANES, LANES), LANES), :] = jnp.zeros((LANES, LANES), F32)


def unpack_block(stage, fpv, q):
    at = pl.multiple_of(q * LANES, LANES)
    stage[pl.ds(at, LANES), :] = fpv[pl.ds(at, LANES), :].astype(F32)


def permute_all(rows, stage, posv, slots, sems, nblk):
    half = nblk // 2

    def load(i, k):
        return pltpu.make_async_copy(posv.at[pl.ds(i * nblk + k * half, half)], slots[k], sems.at[k])

    for k in range(2):
        load(0, k).start()
    last = posv.shape[0] // nblk - 1

    def batch(i, _):
        src = i * (LANES * nblk)
        for k in range(2):
            load(i, k).wait()
            for q in range(half):
                for l in range(LANES):
                    rows[pl.ds(slots[k][q, l], 1), :] = stage[pl.ds(src + l * nblk + k * half + q, 1), :]

            @pl.when(i < last)
            def _():
                load(i + 1, k).start()

        return 0

    lax.fori_loop(0, last + 1, batch, 0)


def convert_all(rows, cap, outs, ends):
    for side in range(2):
        end = jnp.minimum(ends[side], HEAD - LANES)
        blocks = jnp.minimum(lax.shift_right_logical(end + 270, 7), HEAD // LANES)

        def convert(i, _):
            at = pl.multiple_of(i * LANES, LANES)
            src = pl.multiple_of(at + side * cap, LANES)
            outs[side][pl.ds(at, LANES), :] = rows[pl.ds(src, LANES), :].astype(BF16)
            return 0

        lax.fori_loop(0, blocks, convert, 0)


def sort_body(nobs, which, hb, *refs):
    oh_ref, off_ref, cell_ref, fp_ref = refs[:4]
    given = refs[4:4 + 4 * which]
    own_ref, neg_ref, ometa_ref, nmeta_ref = refs[4 + 4 * which:8 + 4 * which]
    fpv, stage, rows, keyv, hourv, posv, slot0, slot1, tabs, tabv, sems = refs[-11:]
    nblk = off_ref.shape[0]
    n = nobs * nblk
    fetch = pltpu.make_async_copy(fp_ref.at[pl.ds(which * n, n)], fpv, sems.at[0])
    fetch.start()
    if which:
        keeps = [pltpu.make_async_copy(given[2 + k], refs[12 + k], sems.at[4 + k]) for k in range(2)]
        for keep in keeps:
            keep.start()
        ometa_ref[:META, :] = given[0][...]
        nmeta_ref[:META, :] = given[1][...]
    sorter = Sorter(nobs, hb, oh_ref, off_ref, cell_ref, (ometa_ref, nmeta_ref), keyv, hourv, posv, tabv)
    cap = sorter.cap

    def aside(phase, r, u):
        if phase == -1:
            fetch.wait()
        elif phase == 0 and u < 3:
            blank_block(rows, cap, r * 6 + u * 2)
            blank_block(rows, cap, r * 6 + u * 2 + 1)
        elif phase == 3:
            unpack_block(stage, fpv, r * 2 + u)

    sorter.prepare(which, aside)
    to_tab = pltpu.make_async_copy(tabv, tabs, sems.at[1])
    to_tab.start()
    permute_all(rows, stage, posv, (slot0, slot1), sems.at[pl.ds(2, 2)], nblk)
    to_tab.wait()
    ends = [tabs[1, k] + tabs[0, k] for k in (CELLS - 1, NBIN - 1)]
    convert_all(rows, cap, (own_ref, neg_ref), ends)
    if which:
        for keep in keeps:
            keep.wait()


def sort_half(oh, off, cell, fp2, which, hb, given=()):
    nblk, count = off.shape
    nobs = count // 2
    n = nobs * nblk
    cap = capacity(n)
    lines = n // LANES
    rows = jax.ShapeDtypeStruct((HEAD, LANES), BF16)
    meta = jax.ShapeDtypeStruct(((1 + which) * META, LANES), I32)
    kept = [jax.ShapeDtypeStruct(v.shape, v.dtype) for v in given[2:]]
    slot = pltpu.SMEM((nblk // 2, LANES), I32)
    return pl.pallas_call(
        functools.partial(sort_body, nobs, which, hb),
        out_shape=(rows, rows, meta, meta, *kept),
        in_specs=[VM, VM, VM, HBM] + ([VM, VM, HBM, HBM] if which else []),
        out_specs=(VM,) * (4 + 2 * which),
        scratch_shapes=[
            pltpu.VMEM((n, LANES), BF16), pltpu.VMEM((n, LANES), F32), pltpu.VMEM((2 * cap, LANES), F32),
            pltpu.VMEM((3, lines, LANES), I32), pltpu.VMEM((lines, LANES), F32), pltpu.VMEM((lines, LANES), I32),
            slot, slot, pltpu.SMEM((8, LANES), I32), pltpu.VMEM((8, LANES), I32), pltpu.SemaphoreType.DMA((6,))],
        compiler_params=pltpu.CompilerParams(vmem_limit_bytes=20 << 20),
        cost_estimate=pl.CostEstimate(flops=10**9, bytes_accessed=50 << 20, transcendentals=0),
        name="sort_half",
    )(oh, off, cell, fp2, *given)


def predict_body(k, slot, chained, *refs):
    flux_ref, rows, meta, tabs = refs[0], refs[1:1 + k], refs[1 + k], refs[2 + k:2 + 2 * k]
    first = [(slot + i) * META for i in range(k)]
    out_ref, tablev = refs[-2:]
    hours = iota((flux_ref.shape[0], k * LANES), 0) + 1
    step = 8

    def group(g, _):
        for u in range(step):
            b = g * step + u
            hour = jnp.concatenate([meta[pl.ds(f + b, 1), :] & 255 for f in first], axis=1)
            fp = jnp.concatenate(
                [rows[i][pl.ds(pl.multiple_of(tabs[i][1, b], 16), LANES), :] for i in range(k)], axis=0)
            local = flux_ref[:, pl.ds(pl.multiple_of(b * LANES, LANES), LANES)]
            full = lax.dot_general(local, fp, NT, preferred_element_type=F32)
            value = jnp.sum(jnp.where(hours == hour, full, 0.0), axis=0, keepdims=True)
            for i in range(k):
                tablev[i, pl.ds(b, 1), :] = value[:, i * LANES:(i + 1) * LANES]
        return 0

    lax.fori_loop(0, CELLS // step, group, 0)
    per = 4
    lines = []
    for i in range(k):
        lo = first[i] + CELLS
        spots = [meta[lo + g * 8:lo + (g + 1) * 8, :] for g in range(8)]
        cell = [lax.shift_right_arithmetic(s, 7) for s in spots]
        lane = [s & 127 for s in spots]

        def collect(q, acc):
            acc = list(acc)
            for u in range(4):
                b = q * 4 + u
                row = jnp.broadcast_to(tablev[i, pl.ds(b, 1), :], (8, LANES))
                for g in range(8):
                    acc[g // 2] = acc[g // 2] + jnp.where(cell[g] == b, pick(row, lane[g]), 0.0)
            return tuple(acc)

        acc = lax.fori_loop(0, CELLS // 4, collect, (jnp.zeros((8, LANES), F32),) * per)
        lines.append(jnp.concatenate([jnp.sum(a, axis=0, keepdims=True) for a in acc], axis=0))
    blank = jnp.zeros((per, LANES), F32)
    if k == 2:
        out_ref[...] = jnp.concatenate(lines, axis=0)
    elif not chained:
        out_ref[...] = jnp.concatenate([lines[0], blank], axis=0)
    else:
        mine_ref, other_ref, tab0_ref, tab1_ref = refs[2 + 2 * k:6 + 2 * k]
        out_ref[0] = mine_ref[...]
        out_ref[1] = jnp.concatenate([blank, lines[0]], axis=0) + other_ref[...]
        out_ref[2] = jnp.maximum(tab0_ref[...], tab1_ref[...]).astype(F32)


def predict(flux, rows, meta, slot=0, more=()):
    k = len(rows)
    tabs = [tab_of(slot + i) for i in range(k)]
    return pl.pallas_call(
        functools.partial(predict_body, k, slot, len(more) > 0),
        grid=(1,),
        out_shape=jax.ShapeDtypeStruct((3, 8, LANES) if more else (8, LANES), F32),
        in_specs=[VM] * (k + 2) + tabs + ([VM, VM, tabv_of(0), tabv_of(1)] if more else []),
        out_specs=VM,
        scratch_shapes=[pltpu.VMEM((k, CELLS, LANES), F32)],
        compiler_params=pltpu.CompilerParams(vmem_limit_bytes=8 << 20),
        cost_estimate=pl.CostEstimate(flops=k * 2 * 240 * 8192 * 128, bytes_accessed=(10 + 5 * k) << 20,
                                      transcendentals=0),
        name="predict",
    )(flux, *rows, meta, *([meta] * k), *more)


def exchange_body(p_ref, value_ref, weight_ref, w_ref, bad_ref, pair, prev_n, next_o, next_obs, flags, mine,
                  s_pair, s_side, s_flag, r_pair, r_side, r_obs, r_flag):
    wins, tiles = lax.axis_size("win"), lax.axis_size("tile")
    w, t = lax.axis_index("win"), lax.axis_index("tile")
    up, down = w > 0, w < wins - 1
    barrier = pltpu.get_barrier_semaphore()
    peers = [lax.rem(t + d, tiles) for d in range(tiles)]
    others = [lax.rem(w + d, wins) for d in range(wins)]

    def greet(device):
        pl.semaphore_signal(barrier, inc=1, device_id=device, device_id_type=MESH)

    for d in range(1, tiles):
        greet((w, peers[d]))
    for d in range(1, wins):
        greet((others[d], t))

    @pl.when(up)
    def _():
        for d in range(1, tiles):
            greet((w - 1, peers[d]))

    @pl.when(down)
    def _():
        for d in range(1, tiles):
            greet((w + 1, peers[d]))

    sides = jnp.where(up, 1, 0) + jnp.where(down, 1, 0)
    pl.semaphore_wait(barrier, tiles - 1 + wins - 1 + sides * (tiles - 1))

    def push(src, dst, ssem, rsem, device):
        return pltpu.make_async_remote_copy(src_ref=src, dst_ref=dst, send_sem=ssem, recv_sem=rsem,
                                            device_id=device, device_id_type=MESH)

    def peer(d, at):
        return push(p_ref, pair.at[at], s_pair.at[d], r_pair.at[at], (w, peers[d]))

    def above(d, at):
        return push(p_ref.at[0], next_o.at[at], s_side.at[0, d], r_side.at[0, at], (w - 1, peers[d]))

    def under(d, at):
        return push(p_ref.at[1], prev_n.at[at], s_side.at[1, d], r_side.at[1, at], (w + 1, peers[d]))

    def obs_to(v):
        return [push(ref, next_obs.at[k], s_side.at[2, k], r_obs.at[k], (v, t))
                for k, ref in enumerate((value_ref, weight_ref))]

    def flag(d, at):
        return push(mine, flags.at[at], s_flag.at[d], r_flag.at[at], (others[d], t))

    for d in range(1, tiles):
        peer(d, t).start()

    @pl.when(up)
    def _():
        for d in range(tiles):
            above(d, t).start()
        for copy in obs_to(w - 1):
            copy.start()

    @pl.when(down)
    def _():
        for d in range(tiles):
            under(d, t).start()

    own, later, bad = p_ref[0], p_ref[1], p_ref[2]
    for d in range(1, tiles):
        peer(d, peers[d]).wait_recv()
        got = pair.at[peers[d]]
        own, later, bad = own + got[0], later + got[1], jnp.maximum(bad, got[2])
    mine[...] = bad
    w_ref[0] = own
    w_ref[1] = later

    @pl.when(up)
    def _():
        total = w_ref[0]
        for d in range(tiles):
            under(d, peers[d]).wait_recv()
            total = total + prev_n[peers[d]]
        w_ref[0] = total

    w_ref[0] = (w_ref[0] - value_ref[...]) * weight_ref[...]
    for d in range(1, wins):
        flag(d, w).start()

    @pl.when(down)
    def _():
        total = w_ref[1]
        for d in range(tiles):
            above(d, peers[d]).wait_recv()
            total = total + next_o[peers[d]]
        for copy in obs_to(w + 1):
            copy.wait_recv()
        w_ref[1] = (total - next_obs[0]) * next_obs[1]

    for d in range(1, wins):
        flag(d, others[d]).wait_recv()
        bad = jnp.maximum(bad, flags[others[d]])
    bad_ref[...] = bad
    for d in range(1, wins):
        flag(d, w).wait_send()
    for d in range(1, tiles):
        peer(d, t).wait_send()

    @pl.when(up)
    def _():
        for copy in obs_to(w - 1):
            copy.wait_send()
        for d in range(tiles):
            above(d, t).wait_send()

    @pl.when(down)
    def _():
        for d in range(tiles):
            under(d, t).wait_send()


def exchange(packet, value, weight):
    wins, tiles = lax.axis_size("win"), lax.axis_size("tile")
    block = pltpu.VMEM((tiles, 8, LANES), F32)
    sem = pltpu.SemaphoreType.DMA
    return pl.pallas_call(
        exchange_body,
        out_shape=(jax.ShapeDtypeStruct((2, 8, LANES), F32), jax.ShapeDtypeStruct((8, LANES), F32)),
        in_specs=[VM, VM, VM],
        out_specs=(VM, VM),
        scratch_shapes=[pltpu.VMEM((tiles, 3, 8, LANES), F32), block, block, pltpu.VMEM((2, 8, LANES), F32),
                        pltpu.VMEM((wins, 8, LANES), F32), pltpu.VMEM((8, LANES), F32),
                        sem((tiles,)), sem((3, tiles)), sem((wins,)), sem((tiles,)), sem((2, tiles)), sem((2,)),
                        sem((wins,))],
        compiler_params=pltpu.CompilerParams(collective_id=3, has_side_effects=True, vmem_limit_bytes=2 << 20),
        name="exchange",
    )(packet, value, weight)


def weigh(code, tables, slots):
    got = [pick(table, lax.shift_right_logical(code, 8) & 127) for table in tables]
    got = got[0] if len(got) == 1 else jnp.where(iota((8, LANES), 1) < 2 * NEAR, got[0], got[1])
    mine = iota((8, LANES), 0) == lax.shift_right_logical(code, 15) + slots
    return jnp.sum(jnp.where(mine, got, 0.0), axis=0, keepdims=True)


def spread(hour, hours, w):
    hit = hours == hour
    return [jnp.where(hit, v, 0.0).astype(BF16) for v in halves(w)]


def edges_body(w_ref, ps_ref, *refs):
    rows, metas, tabs = refs[0:4], refs[4:6], refs[6:10]
    head_ref, tail_ref = refs[10:]
    total = ps_ref.shape[0]
    band = iota((2 * KH, LANES), 0)
    hours = jnp.where(band < KH, band, band + (total - 2 * KH)) + 1
    quarter = lax.shift_right_logical(iota((1, LANES), 1), 5)
    slots = (quarter & 1) * 4
    tables = [w_ref[0], w_ref[1]]

    def group(g, _):
        for u in range(4):
            b = g * 4 + u
            codes = [metas[i // 2][pl.ds((i % 2) * META + b, 1), :] for i in range(4)]
            code = codes[0]
            fps = []
            for i in range(4):
                if i:
                    code = jnp.where(quarter == i, pltpu.roll(codes[i], i * NEAR, 1), code)
                fps.append(rows[i][pl.ds(pl.multiple_of(tabs[i][1, b], 16), NEAR), :])
            fp = jnp.concatenate(fps, axis=0)
            left = jnp.concatenate(spread(code & 255, hours, weigh(code, tables, slots)), axis=1)
            part = dot(left, jnp.concatenate([fp, fp], axis=0))
            col = pl.ds(pl.multiple_of(b * LANES, LANES), LANES)
            head_ref[:, col] = part[:KH] * ps_ref[:KH, col]
            tail_ref[:, col] = part[KH:] * ps_ref[total - KH:, col]
        return 0

    lax.fori_loop(0, CELLS // 4, group, 0)


def edges(w, ps, rows, metas):
    cells = ps.shape[1]
    return pl.pallas_call(
        edges_body,
        grid=(1,),
        out_shape=(jax.ShapeDtypeStruct((KH, cells), F32), jax.ShapeDtypeStruct((KH, cells), F32)),
        in_specs=[VM, VM]
        + [VM] * 4 + [VM] * 2 + [tab_of(0), tab_of(1)] * 2,
        out_specs=(VM, VM),
        compiler_params=pltpu.CompilerParams(vmem_limit_bytes=8 << 20),
        cost_estimate=pl.CostEstimate(flops=10**8, bytes_accessed=8 << 20, transcendentals=0),
        name="edges",
    )(w, ps, *rows, *metas, *tabs_from(metas))


def inner_body(w_ref, head_ref, tail_ref, kern_ref, ps_ref, *refs):
    rows, metas, tabs = refs[0:4], refs[4:6], refs[6:10]
    out_ref, outv, sv, osems = refs[10:]
    total, cells = ps_ref.shape
    parts = 16
    wide = cells // parts
    per = CELLS // parts
    inside = total - 2 * KH

    def drain(p):
        at = pl.ds(pl.multiple_of(p * wide, LANES), wide)
        return pltpu.make_async_copy(outv.at[p & 1], out_ref.at[:, at], osems.at[p & 1])

    hours = iota((inside, LANES), 0) + KH + 1
    pad = jnp.zeros((16, wide), BF16)

    def part_of(p, _):
        for u in range(per):
            b = p * per + u
            left, right = [], []
            for i in range(4):
                code = metas[i // 2][pl.ds((i % 2) * META + b, 1), :]
                left += spread(code & 255, hours, weigh(code, [w_ref[i // 2]], (i % 2) * 4))
                fp = rows[i][pl.ds(pl.multiple_of(tabs[i][1, b], 16), LANES), :]
                right += [fp, fp]
            part = dot(jnp.concatenate(left, axis=1), jnp.concatenate(right, axis=0))
            col = pl.ds(pl.multiple_of(b * LANES, LANES), LANES)
            here = slice(u * LANES, (u + 1) * LANES)
            sv[:KH, here] = head_ref[:, col]
            sv[KH:total - KH, here] = part * ps_ref[KH:total - KH, col]
            sv[total - KH:, here] = tail_ref[:, col]
        top, low = halves(sv[...])
        top, low = top.astype(BF16), low.astype(BF16)
        stack = jnp.concatenate([top, pad, low, pad, top, pad], axis=0)
        smooth = dot(kern_ref[...], stack)

        @pl.when(p >= 2)
        def _():
            drain(p - 2).wait()

        outv[p & 1] = smooth * ps_ref[:, pl.ds(pl.multiple_of(p * wide, LANES), wide)]
        drain(p).start()
        return 0

    lax.fori_loop(0, parts, part_of, 0)
    for p in (parts - 2, parts - 1):
        drain(p).wait()


def inner(w, head, tail, kern, ps, rows, metas):
    wide = ps.shape[1] // 16
    return pl.pallas_call(
        inner_body,
        grid=(1,),
        out_shape=jax.ShapeDtypeStruct(ps.shape, F32),
        in_specs=[VM, VM, VM, VM, VM] + [VM] * 4 + [VM] * 2 + [tab_of(0), tab_of(1)] * 2,
        out_specs=HBM,
        scratch_shapes=[pltpu.VMEM((2, ps.shape[0], wide), F32), pltpu.VMEM((ps.shape[0], wide), F32),
                        pltpu.SemaphoreType.DMA((2,))],
        compiler_params=pltpu.CompilerParams(vmem_limit_bytes=10 << 20),
        cost_estimate=pl.CostEstimate(flops=4 * 10**9, bytes_accessed=40 << 20, transcendentals=0),
        name="inner",
    )(w, head, tail, kern, ps, *rows, *metas, *tabs_from(metas))


def finish_body(own_ref, ps_ref, above_ref, below_ref, out_ref, ownv, loads, stores):
    total = ps_ref.shape[0]
    row = iota((KH, LANES), 0).astype(F32)
    grow, decay = jnp.exp((row - KH) * (2.0 / KH)), jnp.exp(row * (-2.0 / KH))

    def load(side):
        return pltpu.make_async_copy(own_ref.at[pl.ds(side * (total - KH), KH)], ownv.at[side], loads.at[side])

    def store(side):
        return pltpu.make_async_copy(ownv.at[side], out_ref.at[pl.ds(side * (total - KH), KH)], stores.at[side])

    for side in range(2):
        load(side).start()
    for side in range(2):
        load(side).wait()
        scale, after = (grow, decay) if side == 0 else (decay, grow)
        halo_ref = (above_ref, below_ref)[side]
        at = pl.ds(side * (total - KH), KH)

        def fill(q, _):
            for u in range(4):
                cut = pl.ds(pl.multiple_of((q * 4 + u) * LANES, LANES), LANES)
                x = halo_ref[:, cut] * scale
                for s in (1, 2, 4, 8, 16):
                    gap = jnp.zeros((s, LANES), F32)
                    x = x + (jnp.concatenate([gap, x[:KH - s]], axis=0) if side
                             else jnp.concatenate([x[s:], gap], axis=0))
                ownv[side, :, cut] = ownv[side, :, cut] + ps_ref[at, cut] * (x * after)
            return 0

        lax.fori_loop(0, ps_ref.shape[1] // LANES // 4, fill, 0)
        store(side).start()
    for side in range(2):
        store(side).wait()


def finish(partial, ps, above, below):
    return pl.pallas_call(
        finish_body,
        out_shape=jax.ShapeDtypeStruct(ps.shape, F32),
        in_specs=[HBM, VM, VM, VM],
        out_specs=HBM,
        scratch_shapes=[pltpu.VMEM((2, KH, ps.shape[1]), F32), pltpu.SemaphoreType.DMA((2,)),
                        pltpu.SemaphoreType.DMA((2,))],
        input_output_aliases={0: 0},
        compiler_params=pltpu.CompilerParams(vmem_limit_bytes=4 << 20),
        name="finish",
    )(partial, ps, above, below)


def taps(distance):
    far = np.abs(distance)
    full = np.where(far <= KH, np.exp(np.float32(-2.0) * far.astype(np.float32) / np.float32(KH)), 0).astype(np.float32)
    top = full.astype(BF16)
    return top, (full - top.astype(np.float32)).astype(BF16)


def smoother(total):
    row, col = np.arange(total)[:, None], np.arange(256)[None, :]
    top, low = taps(np.where(col < total, row - col, total))
    return jnp.asarray(np.concatenate([top, top, low], axis=1))


def quick(flux, prior_std, w, rows, metas):
    head, tail = edges(w, prior_std, rows, metas)
    above = from_behind(tail, "win", 1)
    below = from_behind(head, "win", -1)
    partial = inner(w, head, tail, smoother(flux.shape[0]), prior_std, rows, metas)
    return finish(partial, prior_std, above, below)


def shards(flux, prior_std, footprint, obs_value, obs_weight, obs_hour, hour_offset, block_cell):
    count, nblk, width = footprint.shape
    inputs = (obs_hour.reshape(1, count), hour_offset.T, block_cell.T, footprint.reshape(count * nblk, width))
    own0, early0, ometa, nmeta = sort_half(*inputs, 0, flux.shape[0])
    theirs0 = from_behind(early0, "win", -1)
    own1, early1, ometa, nmeta, ps, near = sort_half(*inputs, 1, flux.shape[0], (ometa, nmeta, prior_std, flux))
    meta = from_behind(nmeta, "win", -1)
    theirs1 = from_behind(early1, "win", -1)
    mine = predict(near, (own0, own1), ometa)
    other = predict(near, (theirs0,), meta)
    packet = predict(near, (theirs1,), meta, 1, (mine, other, ometa, ometa))
    w, bad = exchange(packet, obs_value.reshape(8, LANES), obs_weight.reshape(8, LANES))
    return lax.cond(
        bad[2, 0] > 0.0,
        lambda: general(flux, prior_std, footprint, obs_value, obs_weight, obs_hour, hour_offset, block_cell),
        lambda: quick(flux, ps, w, [own0, own1, theirs0, theirs1], (ometa, meta)))


def solution(mesh):
    return jax.shard_map(
        shards,
        mesh=mesh,
        in_specs=(
            P("win", "tile"),
            P("win", "tile"),
            P("win", "tile", None),
            P("win"),
            P("win"),
            P("win"),
            P("win", "tile"),
            P("win", "tile"),
        ),
        out_specs=P("win", "tile"),
        check_vma=False,
    )
```

profile of v0, /device:TPU:1, one launch (start us, length us, event | category | flops | bytes accessed | tf_op | source)
XLA Modules:
  0.0 127.0 jit_solution(3325187654269953109)
XLA Ops:
  0.0 16.9 %sort_half.2 = (bf16[5248,128]{1,0:T(8,128)(2,1)S(1)}, bf16[5248,128]{1,0:T(8,128)(2,1)S(1)}, s32[136,128]{1,0:T(8,128)S(1)}, s32[136,128]{1,0:T(8,128)S(1)}) custom-call(s32[1,1024]{1,0:T(1,128)} %bitcast.21, s32[16,1024]{1,0:T(8,128)} %bitcast.17, s32[16,1024]{1,0:T(8,128)} %bitcast.19, bf16[16384,128]{1,0:T(8,128)(2,1)} %bitcast.13), custom_call_target="tpu_custom_call" | custom-call | flops 1000000000 | bytes 52428800 | tf_op jit(solution)/shard_map/sort_half/pallas_call | solution.py:340
  16.9 3.3 %collective-permute-start.8 = (bf16[5248,128]{1,0:T(8,128)(2,1)S(1)}, bf16[5248,128]{1,0:T(8,128)(2,1)S(1)}, u32[]{:S(2)}, u32[]{:S(2)}) collective-permute-start(bf16[5248,128]{1,0:T(8,128)(2,1)S(1)} %get-tuple-element.81), channel_id=1, source_target_pairs={{8,0},{16,8},{24,16},{32,24},{40,32},{48,40},{56,48},{64,56},{72,6... | collective-permute-start | bytes 4030472 | tf_op jit(solution)/shard_map/ppermute | solution.py:58
  20.2 16.9 %sort_half.3 = (bf16[5248,128]{1,0:T(8,128)(2,1)S(1)}, bf16[5248,128]{1,0:T(8,128)(2,1)S(1)}, s32[272,128]{1,0:T(8,128)S(1)}, s32[272,128]{1,0:T(8,128)S(1)}, f3...) custom-call(s32[1,1024]{1,0:T(1,128)} %bitcast.22, s32[16,1024]{1,0:T(8,128)} %bitcast.18, s32[16,1024]{1,0:T(8,128)} %bitcast.20, ...), custom_call_target="tpu_custom_call" | custom-call | flops 1000000000 | bytes 52428800 | tf_op jit(solution)/shard_map/sort_half/pallas_call | solution.py:340
  37.1 1.9 %collective-permute-start.6 = (bf16[5248,128]{1,0:T(8,128)(2,1)S(1)}, bf16[5248,128]{1,0:T(8,128)(2,1)S(1)}, u32[]{:S(2)}, u32[]{:S(2)}) collective-permute-start(bf16[5248,128]{1,0:T(8,128)(2,1)S(1)} %get-tuple-element.76), channel_id=1, source_target_pairs={{8,0},{16,8},{24,16},{32,24},{40,32},{48,40},{56,48},{64,56},{72,6... | collective-permute-start | bytes 4030472 | tf_op jit(solution)/shard_map/ppermute | solution.py:58
  39.0 1.9 %collective-permute-start.7 = (s32[272,128]{1,0:T(8,128)S(1)}, s32[272,128]{1,0:T(8,128)S(1)}, u32[]{:S(2)}, u32[]{:S(2)}) collective-permute-start(s32[272,128]{1,0:T(8,128)S(1)} %get-tuple-element.77), channel_id=1, source_target_pairs={{8,0},{16,8},{24,16},{32,24},{40,32},{48,40},{56,48},{64,56},{72,6... | collective-permute-start | bytes 417800 | tf_op jit(solution)/shard_map/ppermute | solution.py:58
  40.9 0.0 copy-start.4
  40.9 0.0 copy-start.5
  41.0 0.0 copy-start.1
  41.0 0.0 copy-start.2
  41.0 0.0 copy-start.3
  41.0 9.3 %predict.3.refs_4_ = f32[8,128]{1,0:T(8,128)S(1)} custom-call(bf16[240,8192]{1,0:T(8,128)(2,1)S(1)} %get-tuple-element.75.refs_0_, bf16[5248,128]{1,0:T(8,128)(2,1)S(1)} %get-tuple-element.78.refs_1_, bf16[5248,128]{1,0:T(8,128)(2,1)S(1)} %get-tuple-element.79.refs_2_, s32[272,128]{1,0:T(8,128)S(1)} %get-tuple-element.80.refs_3_.refs_4_.refs_5_.refs_6_.refs_7_, ...), custom_call_target="tpu_custom_call" | custom-call | flops 1006632960 | bytes 20971520 | tf_op jit(solution)/shard_map/predict/pallas_call | solution.py:410
  50.3 9.1 %collective-permute-done.7.refs_2_.refs_3_ = s32[272,128]{1,0:T(8,128)S(1)} collective-permute-done((s32[272,128]{1,0:T(8,128)S(1)}, s32[272,128]{1,0:T(8,128)S(1)}, u32[]{:S(2)}, u32[]{:S(2)}) %collective-permute-start.7) | collective-permute-done | bytes 139296 | tf_op jit(solution)/shard_map/ppermute | solution.py:58
  59.4 0.0 collective-permute-done.8.refs_1_
  59.4 6.7 %predict.4.refs_5_ = f32[8,128]{1,0:T(8,128)S(1)} custom-call(bf16[240,8192]{1,0:T(8,128)(2,1)S(1)} %get-tuple-element.75.refs_0_, bf16[5248,128]{1,0:T(8,128)(2,1)S(1)} %collective-permute-done.8.refs_1_, s32[272,128]{1,0:T(8,128)S(1)} %collective-permute-done.7.refs_2_.refs_3_, s32[272,128]{1,0:T(8,128)S(1)} %collective-permute-done.7.refs_2_.refs_3_), custom_call_target="tpu_custom_call" | custom-call | flops 503316480 | bytes 15728640 | tf_op jit(solution)/shard_map/predict/pallas_call | solution.py:410
  66.0 0.0 collective-permute-done.6.refs_1_
  66.0 6.7 %predict.5.p_ref = f32[3,8,128]{2,1,0:T(8,128)S(1)} custom-call(bf16[240,8192]{1,0:T(8,128)(2,1)S(1)} %get-tuple-element.75.refs_0_, bf16[5248,128]{1,0:T(8,128)(2,1)S(1)} %collective-permute-done.6.refs_1_, s32[272,128]{1,0:T(8,128)S(1)} %collective-permute-done.7.refs_2_.refs_3_, s32[272,128]{1,0:T(8,128)S(1)} %collective-permute-done.7.refs_2_.refs_3_, ...), custom_call_target="tpu_custom_call" | custom-call | flops 503316480 | bytes 15728640 | tf_op jit(solution)/shard_map/predict/pallas_call | solution.py:410
  72.7 0.0 copy-done.4
  72.7 0.0 copy-done.5
  72.7 18.5 %exchange.1 = (f32[2,8,128]{2,1,0:T(8,128)S(1)}, f32[8,128]{1,0:T(8,128)S(1)}) custom-call(f32[3,8,128]{2,1,0:T(8,128)S(1)} %predict.5.p_ref, f32[8,128]{1,0:T(8,128)S(1)} %bitcast.23, f32[8,128]{1,0:T(8,128)S(1)} %bitcast.24), custom_call_target="tpu_custom_call" | custom-call | tf_op jit(solution)/shard_map/exchange/pallas_call | solution.py:546
  91.3 0.5 slice.21
  92.4 0.0 copy-done.1
  92.4 0.0 copy-done.2
  92.4 0.0 copy-done.3
  92.4 34.3 %conditional.1 = (f32[240,8192]{1,0:T(8,128)}) conditional(s32[]{:T(128)} %bitcast.11, (f32[2,8,128]{2,1,0:T(8,128)S(1)}, f32[240,8192]{1,0:T(8,128)S(1)}, bf16[5248,128]{1,0:T(8,128)(2,1)S(1)}, bf16[5248,128]{1,0:T(8,128)(2,1)S(1)}, bf16[5248,128]{1,0:T(8,128)(2,1)S(1)}, /*index=5*/bf16[5248,128]{1,0:T(8,128)(2,1)S(1)}, s32[272,128]{1,0:T(8,128)S(1)}, ...), branch_computations={%region_0.0_spmd, %region_1.4_spmd} | conditional | flops 6836399616 | bytes 253735552 | solution.py:766
  92.5 0.0 copy-start
  92.5 5.9 %edges.1 = (f32[24,8192]{1,0:T(8,128)S(1)}, f32[24,8192]{1,0:T(8,128)S(1)}) custom-call(f32[2,8,128]{2,1,0:T(8,128)S(1)} %get-tuple-element.42.w_ref, f32[240,8192]{1,0:T(8,128)S(1)} %get-tuple-element.43.ps_ref, bf16[5248,128]{1,0:T(8,128)(2,1)S(1)} %get-tuple-element.44.refs_0_, bf16[5248,128]{1,0:T(8,128)(2,1)S(1)} %get-tuple-element.45.refs_1_, ...), custom_call_target="tpu_custom_call" | custom-call | flops 100000000 | bytes 8388608 | tf_op jit(solution)/shard_map/cond/branch_0_fun/edges/pallas_call | solution.py:605
  98.4 2.3 %collective-permute-start.1 = (f32[24,8192]{1,0:T(8,128)S(1)}, f32[24,8192]{1,0:T(8,128)S(1)}, u32[]{:S(2)}, u32[]{:S(2)}) collective-permute-start(f32[24,8192]{1,0:T(8,128)S(1)} %get-tuple-element.50.head_ref), channel_id=1, source_target_pairs={{8,0},{16,8},{24,16},{32,24},{40,32},{48,40},{56,48},{64,56},{72,6... | collective-permute-start | bytes 2359304 | tf_op jit(solution)/shard_map/cond/branch_0_fun/ppermute | solution.py:58
  100.7 4.8 %collective-permute-start = (f32[24,8192]{1,0:T(8,128)S(1)}, f32[24,8192]{1,0:T(8,128)S(1)}, u32[]{:S(2)}, u32[]{:S(2)}) collective-permute-start(f32[24,8192]{1,0:T(8,128)S(1)} %get-tuple-element.51.tail_ref), channel_id=1, source_target_pairs={{0,8},{8,16},{16,24},{24,32},{32,40},{40,48},{48,56},{56,64},{64,7... | collective-permute-start | bytes 2359304 | tf_op jit(solution)/shard_map/cond/branch_0_fun/ppermute | solution.py:58
  105.5 0.0 copy-done
  105.5 17.8 %inner.1.own_ref = f32[240,8192]{1,0:T(8,128)} custom-call(f32[2,8,128]{2,1,0:T(8,128)S(1)} %get-tuple-element.42.w_ref, f32[24,8192]{1,0:T(8,128)S(1)} %get-tuple-element.50.head_ref, f32[24,8192]{1,0:T(8,128)S(1)} %get-tuple-element.51.tail_ref, bf16[240,768]{1,0:T(8,128)(2,1)S(1)} %copy-done, f32[240,8192]{1,0:T(8,128)S(1)} %get-tuple-element.43.ps_ref, ...), custom_call_target="tpu_custom_call" | custom-call | flops 4000000000 | bytes 41943040 | tf_op jit(solution)/shard_map/cond/branch_0_fun/inner/pallas_call | solution.py:669
  123.3 0.0 collective-permute-done.1.below_ref
  123.3 0.0 collective-permute-done.above_ref
  123.3 3.1 %finish.1 = f32[240,8192]{1,0:T(8,128)} custom-call(f32[240,8192]{1,0:T(8,128)} %inner.1.own_ref, f32[240,8192]{1,0:T(8,128)S(1)} %get-tuple-element.43.ps_ref, f32[24,8192]{1,0:T(8,128)S(1)} %collective-permute-done.above_ref, f32[24,8192]{1,0:T(8,128)S(1)} %collective-permute-done.1.below_ref), custom_call_target="tpu_custom_call", output_to_operand_aliasing={{}: (0, {})} | custom-call | tf_op jit(solution)/shard_map/cond/branch_0_fun/finish/pallas_call | solution.py:720
Async XLA Ops:
  16.9 42.5 %collective-permute-start.8 = (bf16[5248,128]{1,0:T(8,128)(2,1)S(1)}, bf16[5248,128]{1,0:T(8,128)(2,1)S(1)}, u32[]{:S(2)}, u32[]{:S(2)}) collective-permute-start(bf16[5248,128]{1,0:T(8,128)(2,1)S(1)} %get-tuple-element.81), channel_id=1, source_target_pairs={{8,0},{16,8},{24,16},{32,24},{40,32},{48,40},{56,48},{64,56},{72,6... | collective-permute-start | bytes 4030472 | tf_op jit(solution)/shard_map/ppermute | solution.py:58
  37.1 28.9 %collective-permute-start.6 = (bf16[5248,128]{1,0:T(8,128)(2,1)S(1)}, bf16[5248,128]{1,0:T(8,128)(2,1)S(1)}, u32[]{:S(2)}, u32[]{:S(2)}) collective-permute-start(bf16[5248,128]{1,0:T(8,128)(2,1)S(1)} %get-tuple-element.76), channel_id=1, source_target_pairs={{8,0},{16,8},{24,16},{32,24},{40,32},{48,40},{56,48},{64,56},{72,6... | collective-permute-start | bytes 4030472 | tf_op jit(solution)/shard_map/ppermute | solution.py:58
  39.0 20.3 %collective-permute-start.7 = (s32[272,128]{1,0:T(8,128)S(1)}, s32[272,128]{1,0:T(8,128)S(1)}, u32[]{:S(2)}, u32[]{:S(2)}) collective-permute-start(s32[272,128]{1,0:T(8,128)S(1)} %get-tuple-element.77), channel_id=1, source_target_pairs={{8,0},{16,8},{24,16},{32,24},{40,32},{48,40},{56,48},{64,56},{72,6... | collective-permute-start | bytes 417800 | tf_op jit(solution)/shard_map/ppermute | solution.py:58
  40.9 31.8 %copy-start.4 = (f32[1024]{0:T(1024)S(1)}, f32[1024]{0:T(1024)}, u32[]{:S(2)}) copy-start(f32[1024]{0:T(1024)} %param.14) | copy-start | bytes 12292
  40.9 31.8 %copy-start.5 = (f32[1024]{0:T(1024)S(1)}, f32[1024]{0:T(1024)}, u32[]{:S(2)}) copy-start(f32[1024]{0:T(1024)} %param.15) | copy-start | bytes 12292
  41.0 51.5 %copy-start.1 = (s32[1024,16]{0,1:T(8,128)S(1)}, s32[1024,16]{0,1:T(8,128)}, u32[]{:S(2)}) copy-start(s32[1024,16]{0,1:T(8,128)} %param.17) | copy-start | bytes 196612
  41.0 51.5 %copy-start.2 = (s32[1024,16]{0,1:T(8,128)S(1)}, s32[1024,16]{0,1:T(8,128)}, u32[]{:S(2)}) copy-start(s32[1024,16]{0,1:T(8,128)} %param.18) | copy-start | bytes 196612
  41.0 51.5 %copy-start.3 = (s32[1024]{0:T(1024)S(1)}, s32[1024]{0:T(1024)}, u32[]{:S(2)}) copy-start(s32[1024]{0:T(1024)} %param.16) | copy-start | bytes 12292
  92.5 13.0 %copy-start = (bf16[240,768]{1,0:T(8,128)(2,1)S(1)}, bf16[240,768]{1,0:T(8,128)(2,1)}, u32[]{:S(2)}) copy-start(bf16[240,768]{1,0:T(8,128)(2,1)} %constant.25.clone.1.kern_ref) | copy-start | bytes 1105924 | tf_op jit(solution)/shard_map/cond
  98.4 24.9 %collective-permute-start.1 = (f32[24,8192]{1,0:T(8,128)S(1)}, f32[24,8192]{1,0:T(8,128)S(1)}, u32[]{:S(2)}, u32[]{:S(2)}) collective-permute-start(f32[24,8192]{1,0:T(8,128)S(1)} %get-tuple-element.50.head_ref), channel_id=1, source_target_pairs={{8,0},{16,8},{24,16},{32,24},{40,32},{48,40},{56,48},{64,56},{72,6... | collective-permute-start | bytes 2359304 | tf_op jit(solution)/shard_map/cond/branch_0_fun/ppermute | solution.py:58
  100.7 22.7 %collective-permute-start = (f32[24,8192]{1,0:T(8,128)S(1)}, f32[24,8192]{1,0:T(8,128)S(1)}, u32[]{:S(2)}, u32[]{:S(2)}) collective-permute-start(f32[24,8192]{1,0:T(8,128)S(1)} %get-tuple-element.51.tail_ref), channel_id=1, source_target_pairs={{0,8},{8,16},{16,24},{24,32},{32,40},{40,48},{48,56},{56,64},{64,7... | collective-permute-start | bytes 2359304 | tf_op jit(solution)/shard_map/cond/branch_0_fun/ppermute | solution.py:58
where the time goes:
time: 127 us
  Pallas kernels  102 us (80%)
  starting transfers between devices  14.2 us (11%)
  waiting for transfers between devices  9.09 us (7%)
    pallas_call x2, Pallas kernels, sort_half(): pl.pallas_call(functools.partial(sort_body, nobs, which, hb), out_shape=(...  33.8 us
    pallas_call x3, Pallas kernels, predict(): pl.pallas_call(functools.partial(predict_body, k, slot, len(more) > 0), g...  22.6 us
    pallas_call x1, Pallas kernels, exchange(): pl.pallas_call(exchange_body, out_shape=(jax.ShapeDtypeStruct((2, 8, LANE...  18.5 us
    pallas_call x1, Pallas kernels, inner(): pl.pallas_call(inner_body, grid=(1,), out_shape=jax.ShapeDtypeStruct(ps.s...  17.8 us
    ppermute x5, starting transfers between devices, from_behind(): lax.ppermute(value, axis, [(source, source + steps) for source in range(i...  14.2 us
    ppermute x5, waiting for transfers between devices, from_behind(): lax.ppermute(value, axis, [(source, source + steps) for source in range(i...  9.09 us
    pallas_call x1, Pallas kernels, edges(): pl.pallas_call(edges_body, grid=(1,), out_shape=(jax.ShapeDtypeStruct((KH...  5.89 us
    pallas_call x1, Pallas kernels, finish(): pl.pallas_call(finish_body, out_shape=jax.ShapeDtypeStruct(ps.shape, F32)...  3.14 us
  transfers between devices with their start and end apart: 5, of which 1 were waited for; matrix products, arithmetic and copies ran while one was open for 0% of the time, Pallas kernels for 40%

commit v1 on v0

--- a/solution.py
+++ b/solution.py
@@ -352,10 +352,8 @@
     )(oh, off, cell, fp2, *given)
 
 
-def predict_body(k, slot, chained, *refs):
-    flux_ref, rows, meta, tabs = refs[0], refs[1:1 + k], refs[1 + k], refs[2 + k:2 + 2 * k]
-    first = [(slot + i) * META for i in range(k)]
-    out_ref, tablev = refs[-2:]
+def predict_cells(flux_ref, rows, meta, tabs, first, tablev):
+    k = len(rows)
     hours = iota((flux_ref.shape[0], k * LANES), 0) + 1
     step = 8
 
@@ -373,9 +371,11 @@
         return 0
 
     lax.fori_loop(0, CELLS // step, group, 0)
-    per = 4
+
+
+def predict_sums(meta, first, tablev):
     lines = []
-    for i in range(k):
+    for i in range(len(first)):
         lo = first[i] + CELLS
         spots = [meta[lo + g * 8:lo + (g + 1) * 8, :] for g in range(8)]
         cell = [lax.shift_right_arithmetic(s, 7) for s in spots]
@@ -390,39 +390,65 @@
                     acc[g // 2] = acc[g // 2] + jnp.where(cell[g] == b, pick(row, lane[g]), 0.0)
             return tuple(acc)
 
-        acc = lax.fori_loop(0, CELLS // 4, collect, (jnp.zeros((8, LANES), F32),) * per)
+        acc = lax.fori_loop(0, CELLS // 4, collect, (jnp.zeros((8, LANES), F32),) * 4)
         lines.append(jnp.concatenate([jnp.sum(a, axis=0, keepdims=True) for a in acc], axis=0))
-    blank = jnp.zeros((per, LANES), F32)
-    if k == 2:
-        out_ref[...] = jnp.concatenate(lines, axis=0)
-    elif not chained:
-        out_ref[...] = jnp.concatenate([lines[0], blank], axis=0)
-    else:
-        mine_ref, other_ref, tab0_ref, tab1_ref = refs[2 + 2 * k:6 + 2 * k]
-        out_ref[0] = mine_ref[...]
-        out_ref[1] = jnp.concatenate([blank, lines[0]], axis=0) + other_ref[...]
-        out_ref[2] = jnp.maximum(tab0_ref[...], tab1_ref[...]).astype(F32)
-
-
-def predict(flux, rows, meta, slot=0, more=()):
+    return lines
+
+
+def predict_binned(flux_ref, rows_ref, meta_ref, first):
+    hours = iota((flux_ref.shape[0], LANES), 0) + 1
+    eight, bins = iota((8, LANES), 0), iota((LANES, LANES), 0)
+    step = 8
+
+    def group(g, acc):
+        left, right = [], []
+        for u in range(step):
+            b = g * step + u
+            code = meta_ref[pl.ds(first + b, 1), :]
+            fp = rows_ref[pl.ds(pl.multiple_of(b * LANES, LANES), LANES), :]
+            local = flux_ref[:, pl.ds(pl.multiple_of(b * LANES, LANES), LANES)]
+            full = lax.dot_general(local, fp, NT, preferred_element_type=F32)
+            value = jnp.sum(jnp.where(hours == (code & 255), full, 0.0), axis=0, keepdims=True)
+            here = eight == lax.shift_right_logical(code, 15)
+            left.append(jnp.concatenate([jnp.where(here, v, 0.0) for v in halves(value)], axis=0).astype(BF16))
+            right.append(jnp.where(bins == (lax.shift_right_logical(code, 8) & 127), 1.0, 0.0).astype(BF16))
+        for at in range(0, step, 2):
+            acc = acc + lax.dot_general(jnp.concatenate(left[at:at + 2], axis=1),
+                                        jnp.concatenate(right[at:at + 2], axis=1), NT, preferred_element_type=F32)
+        return acc
+
+    acc = lax.fori_loop(0, CELLS // step, group, jnp.zeros((16, LANES), F32))
+    return acc[:4] + acc[8:12]
+
+
+def predict_body(k, *refs):
+    flux_ref, rows, meta, tabs = refs[0], refs[1:1 + k], refs[1 + k], refs[2 + k:2 + 2 * k]
+    out_ref, tablev = refs[-2:]
+    first = [i * META for i in range(k)]
+    predict_cells(flux_ref, rows, meta, tabs, first, tablev)
+    lines = predict_sums(meta, first, tablev)
+    out_ref[...] = jnp.concatenate(lines if k == 2 else lines + [jnp.zeros((4, LANES), F32)], axis=0)
+
+
+def predict(flux, rows, meta):
     k = len(rows)
-    tabs = [tab_of(slot + i) for i in range(k)]
     return pl.pallas_call(
-        functools.partial(predict_body, k, slot, len(more) > 0),
+        functools.partial(predict_body, k),
         grid=(1,),
-        out_shape=jax.ShapeDtypeStruct((3, 8, LANES) if more else (8, LANES), F32),
-        in_specs=[VM] * (k + 2) + tabs + ([VM, VM, tabv_of(0), tabv_of(1)] if more else []),
+        out_shape=jax.ShapeDtypeStruct((8, LANES), F32),
+        in_specs=[VM] * (k + 2) + [tab_of(i) for i in range(k)],
         out_specs=VM,
         scratch_shapes=[pltpu.VMEM((k, CELLS, LANES), F32)],
         compiler_params=pltpu.CompilerParams(vmem_limit_bytes=8 << 20),
         cost_estimate=pl.CostEstimate(flops=k * 2 * 240 * 8192 * 128, bytes_accessed=(10 + 5 * k) << 20,
                                       transcendentals=0),
         name="predict",
-    )(flux, *rows, meta, *([meta] * k), *more)
-
-
-def exchange_body(p_ref, value_ref, weight_ref, w_ref, bad_ref, pair, prev_n, next_o, next_obs, flags, mine,
-                  s_pair, s_side, s_flag, r_pair, r_side, r_obs, r_flag):
+    )(flux, *rows, meta, *([meta] * k))
+
+
+def exchange_body(flux_ref, rows_ref, meta_ref, mine_ref, other_ref, tab0_ref, tab1_ref, value_ref,
+                  weight_ref, w_ref, bad_ref, later_ref, flag0, flag1, pair_o, pair_n, pair_f, prev_n, next_o,
+                  next_obs, flags, s_pair, s_side, s_obs, s_flag, r_pair, r_side, r_obs, r_flag):
     wins, tiles = lax.axis_size("win"), lax.axis_size("tile")
     w, t = lax.axis_index("win"), lax.axis_index("tile")
     up, down = w > 0, w < wins - 1
@@ -448,6 +474,10 @@
         for d in range(1, tiles):
             greet((w + 1, peers[d]))
 
+    flag0[...] = jnp.maximum(tab0_ref[...], tab1_ref[...]).astype(F32)
+    lines = predict_binned(flux_ref, rows_ref, meta_ref, META)
+    later = jnp.concatenate([jnp.zeros((4, LANES), F32), lines], axis=0) + other_ref[...]
+    later_ref[...] = later
     sides = jnp.where(up, 1, 0) + jnp.where(down, 1, 0)
     pl.semaphore_wait(barrier, tiles - 1 + wins - 1 + sides * (tiles - 1))
 
@@ -455,24 +485,27 @@
         return pltpu.make_async_remote_copy(src_ref=src, dst_ref=dst, send_sem=ssem, recv_sem=rsem,
                                             device_id=device, device_id_type=MESH)
 
-    def peer(d, at):
-        return push(p_ref, pair.at[at], s_pair.at[d], r_pair.at[at], (w, peers[d]))
+    def peer(k, d, at):
+        src, dst = ((mine_ref, pair_o), (later_ref, pair_n), (flag0, pair_f))[k]
+        return push(src, dst.at[at], s_pair.at[k, d], r_pair.at[k, at], (w, peers[d]))
 
     def above(d, at):
-        return push(p_ref.at[0], next_o.at[at], s_side.at[0, d], r_side.at[0, at], (w - 1, peers[d]))
+        return push(mine_ref, next_o.at[at], s_side.at[0, d], r_side.at[0, at], (w - 1, peers[d]))
 
     def under(d, at):
-        return push(p_ref.at[1], prev_n.at[at], s_side.at[1, d], r_side.at[1, at], (w + 1, peers[d]))
+        return push(later_ref, prev_n.at[at], s_side.at[1, d], r_side.at[1, at], (w + 1, peers[d]))
 
     def obs_to(v):
-        return [push(ref, next_obs.at[k], s_side.at[2, k], r_obs.at[k], (v, t))
+        return [push(ref, next_obs.at[k], s_obs.at[k], r_obs.at[k], (v, t))
                 for k, ref in enumerate((value_ref, weight_ref))]
 
     def flag(d, at):
-        return push(mine, flags.at[at], s_flag.at[d], r_flag.at[at], (others[d], t))
+        return push(flag1, flags.at[at], s_flag.at[d], r_flag.at[at], (others[d], t))
 
     for d in range(1, tiles):
-        peer(d, t).start()
+        peer(2, d, t).start()
+    for d in range(1, tiles):
+        peer(0, d, t).start()
 
     @pl.when(up)
     def _():
@@ -481,17 +514,26 @@
         for copy in obs_to(w - 1):
             copy.start()
 
+    for d in range(1, tiles):
+        peer(1, d, t).start()
+
     @pl.when(down)
     def _():
         for d in range(tiles):
             under(d, t).start()
 
-    own, later, bad = p_ref[0], p_ref[1], p_ref[2]
+    bad = flag0[...]
     for d in range(1, tiles):
-        peer(d, peers[d]).wait_recv()
-        got = pair.at[peers[d]]
-        own, later, bad = own + got[0], later + got[1], jnp.maximum(bad, got[2])
-    mine[...] = bad
+        peer(2, d, peers[d]).wait_recv()
+        bad = jnp.maximum(bad, pair_f[peers[d]])
+    flag1[...] = bad
+    for d in range(1, wins):
+        flag(d, w).start()
+    own = mine_ref[...]
+    for d in range(1, tiles):
+        for k in range(2):
+            peer(k, d, peers[d]).wait_recv()
+        own, later = own + pair_o[peers[d]], later + pair_n[peers[d]]
     w_ref[0] = own
     w_ref[1] = later
 
@@ -504,8 +546,6 @@
         w_ref[0] = total
 
     w_ref[0] = (w_ref[0] - value_ref[...]) * weight_ref[...]
-    for d in range(1, wins):
-        flag(d, w).start()
 
     @pl.when(down)
     def _():
@@ -524,7 +564,8 @@
     for d in range(1, wins):
         flag(d, w).wait_send()
     for d in range(1, tiles):
-        peer(d, t).wait_send()
+        for k in range(3):
+            peer(k, d, t).wait_send()
 
     @pl.when(up)
     def _():
@@ -539,22 +580,48 @@
             under(d, t).wait_send()
 
 
-def exchange(packet, value, weight):
+def align_body(rows_ref, tab_ref, out_ref):
+    def move(q, _):
+        for u in range(4):
+            b = q * 4 + u
+            at = pl.ds(pl.multiple_of(tab_ref[1, b], 16), LANES)
+            out_ref[pl.ds(pl.multiple_of(b * LANES, LANES), LANES), :] = rows_ref[at, :]
+        return 0
+
+    lax.fori_loop(0, CELLS // 4, move, 0)
+
+
+def align(rows, meta):
+    return pl.pallas_call(
+        align_body,
+        grid=(1,),
+        out_shape=jax.ShapeDtypeStruct((CELLS * LANES, LANES), BF16),
+        in_specs=[VM, tab_of(1)],
+        out_specs=VM,
+        compiler_params=pltpu.CompilerParams(vmem_limit_bytes=2 << 20),
+        name="align",
+    )(rows, meta)
+
+
+def exchange(flux, rows, meta, mine, other, ometa, value, weight):
     wins, tiles = lax.axis_size("win"), lax.axis_size("tile")
+    one = pltpu.VMEM((8, LANES), F32)
     block = pltpu.VMEM((tiles, 8, LANES), F32)
     sem = pltpu.SemaphoreType.DMA
     return pl.pallas_call(
         exchange_body,
+        grid=(1,),
         out_shape=(jax.ShapeDtypeStruct((2, 8, LANES), F32), jax.ShapeDtypeStruct((8, LANES), F32)),
-        in_specs=[VM, VM, VM],
+        in_specs=[VM, VM, VM, VM, VM, tabv_of(0), tabv_of(1), VM, VM],
         out_specs=(VM, VM),
-        scratch_shapes=[pltpu.VMEM((tiles, 3, 8, LANES), F32), block, block, pltpu.VMEM((2, 8, LANES), F32),
-                        pltpu.VMEM((wins, 8, LANES), F32), pltpu.VMEM((8, LANES), F32),
-                        sem((tiles,)), sem((3, tiles)), sem((wins,)), sem((tiles,)), sem((2, tiles)), sem((2,)),
-                        sem((wins,))],
-        compiler_params=pltpu.CompilerParams(collective_id=3, has_side_effects=True, vmem_limit_bytes=2 << 20),
+        scratch_shapes=[one, one, one, block, block, block, block, block,
+                        pltpu.VMEM((2, 8, LANES), F32), pltpu.VMEM((wins, 8, LANES), F32),
+                        sem((3, tiles)), sem((2, tiles)), sem((2,)), sem((wins,)), sem((3, tiles)), sem((2, tiles)),
+                        sem((2,)), sem((wins,))],
+        compiler_params=pltpu.CompilerParams(collective_id=3, has_side_effects=True, vmem_limit_bytes=8 << 20),
+        cost_estimate=pl.CostEstimate(flops=2 * 240 * 8192 * 128, bytes_accessed=30 << 20, transcendentals=0),
         name="exchange",
-    )(packet, value, weight)
+    )(flux, align(rows, meta), meta, mine, other, ometa, ometa, value, weight)
 
 
 def weigh(code, tables, slots):
@@ -761,8 +828,8 @@
     theirs1 = from_behind(early1, "win", -1)
     mine = predict(near, (own0, own1), ometa)
     other = predict(near, (theirs0,), meta)
-    packet = predict(near, (theirs1,), meta, 1, (mine, other, ometa, ometa))
-    w, bad = exchange(packet, obs_value.reshape(8, LANES), obs_weight.reshape(8, LANES))
+    w, bad = exchange(near, theirs1, meta, mine, other, ometa, obs_value.reshape(8, LANES),
+                      obs_weight.reshape(8, LANES))
     return lax.cond(
         bad[2, 0] > 0.0,
         lambda: general(flux, prior_std, footprint, obs_value, obs_weight, obs_hour, hour_offset, block_cell),

time: 127 us -> 123 us (0.969)
  Pallas kernels: 102 us -> 97.4 us
    pallas_call x4, Pallas kernels: 41.1 us -> 36.8 us  [the longest x1 19.9 us: exchange(): pl.pallas_call(exchange_body, grid=(1,), out_shape=(jax.ShapeDtypeStruct(...]
  transfers between devices with their start and end apart: 5 -> 5, of which waited for: 1 -> 1; matrix products, arithmetic and copies ran while one was open for 0% -> 0% of each run, Pallas kernels for 40% -> 41%
where the time goes in v1:
time: 123 us
  Pallas kernels  97.4 us (79%)
  starting transfers between devices  14.2 us (12%)
  waiting for transfers between devices  9.1 us (7%)
    pallas_call x2, Pallas kernels, sort_half(): pl.pallas_call(functools.partial(sort_body, nobs, which, hb), out_shape=(...  33.8 us
    pallas_call x1, Pallas kernels, exchange(): pl.pallas_call(exchange_body, grid=(1,), out_shape=(jax.ShapeDtypeStruct(...  19.9 us
    pallas_call x1, Pallas kernels, inner(): pl.pallas_call(inner_body, grid=(1,), out_shape=jax.ShapeDtypeStruct(ps.s...  17.9 us
    pallas_call x2, Pallas kernels, predict(): pl.pallas_call(functools.partial(predict_body, k), grid=(1,), out_shape=j...  15.9 us
    ppermute x5, starting transfers between devices, from_behind(): lax.ppermute(value, axis, [(source, source + steps) for source in range(i...  14.2 us
    ppermute x5, waiting for transfers between devices, from_behind(): lax.ppermute(value, axis, [(source, source + steps) for source in range(i...  9.1 us
    pallas_call x1, Pallas kernels, edges(): pl.pallas_call(edges_body, grid=(1,), out_shape=(jax.ShapeDtypeStruct((KH...  5.89 us
    pallas_call x1, Pallas kernels, finish(): pl.pallas_call(finish_body, out_shape=jax.ShapeDtypeStruct(ps.shape, F32)...  3.14 us
  transfers between devices with their start and end apart: 5, of which 1 were waited for; matrix products, arithmetic and copies ran while one was open for 0% of the time, Pallas kernels for 41%

profile of v1, /device:TPU:1, one launch (start us, length us, event | category | flops | bytes accessed | tf_op | source)
XLA Modules:
  0.0 122.6 jit_solution(14699150094209515668)
XLA Ops:
  0.0 16.9 %sort_half.2 = (bf16[5248,128]{1,0:T(8,128)(2,1)S(1)}, bf16[5248,128]{1,0:T(8,128)(2,1)S(1)}, s32[136,128]{1,0:T(8,128)S(1)}, s32[136,128]{1,0:T(8,128)S(1)}) custom-call(s32[1,1024]{1,0:T(1,128)} %bitcast.21, s32[16,1024]{1,0:T(8,128)} %bitcast.17, s32[16,1024]{1,0:T(8,128)} %bitcast.19, bf16[16384,128]{1,0:T(8,128)(2,1)} %bitcast.13), custom_call_target="tpu_custom_call" | custom-call | flops 1000000000 | bytes 52428800 | tf_op jit(solution)/shard_map/sort_half/pallas_call | solution.py:340
  16.9 3.3 %collective-permute-start.8 = (bf16[5248,128]{1,0:T(8,128)(2,1)S(1)}, bf16[5248,128]{1,0:T(8,128)(2,1)S(1)}, u32[]{:S(2)}, u32[]{:S(2)}) collective-permute-start(bf16[5248,128]{1,0:T(8,128)(2,1)S(1)} %get-tuple-element.81), channel_id=1, source_target_pairs={{8,0},{16,8},{24,16},{32,24},{40,32},{48,40},{56,48},{64,56},{72,6... | collective-permute-start | bytes 4030472 | tf_op jit(solution)/shard_map/ppermute | solution.py:58
  20.2 16.9 %sort_half.3 = (bf16[5248,128]{1,0:T(8,128)(2,1)S(1)}, bf16[5248,128]{1,0:T(8,128)(2,1)S(1)}, s32[272,128]{1,0:T(8,128)S(1)}, s32[272,128]{1,0:T(8,128)S(1)}, f3...) custom-call(s32[1,1024]{1,0:T(1,128)} %bitcast.22, s32[16,1024]{1,0:T(8,128)} %bitcast.18, s32[16,1024]{1,0:T(8,128)} %bitcast.20, ...), custom_call_target="tpu_custom_call" | custom-call | flops 1000000000 | bytes 52428800 | tf_op jit(solution)/shard_map/sort_half/pallas_call | solution.py:340
  37.1 1.9 %collective-permute-start.6 = (bf16[5248,128]{1,0:T(8,128)(2,1)S(1)}, bf16[5248,128]{1,0:T(8,128)(2,1)S(1)}, u32[]{:S(2)}, u32[]{:S(2)}) collective-permute-start(bf16[5248,128]{1,0:T(8,128)(2,1)S(1)} %get-tuple-element.76), channel_id=1, source_target_pairs={{8,0},{16,8},{24,16},{32,24},{40,32},{48,40},{56,48},{64,56},{72,6... | collective-permute-start | bytes 4030472 | tf_op jit(solution)/shard_map/ppermute | solution.py:58
  39.0 1.9 %collective-permute-start.7 = (s32[272,128]{1,0:T(8,128)S(1)}, s32[272,128]{1,0:T(8,128)S(1)}, u32[]{:S(2)}, u32[]{:S(2)}) collective-permute-start(s32[272,128]{1,0:T(8,128)S(1)} %get-tuple-element.77), channel_id=1, source_target_pairs={{8,0},{16,8},{24,16},{32,24},{40,32},{48,40},{56,48},{64,56},{72,6... | collective-permute-start | bytes 417800 | tf_op jit(solution)/shard_map/ppermute | solution.py:58
  40.9 0.0 copy-start.4
  40.9 0.0 copy-start.5
  41.0 9.3 %predict.2.mine_ref = f32[8,128]{1,0:T(8,128)S(1)} custom-call(bf16[240,8192]{1,0:T(8,128)(2,1)S(1)} %get-tuple-element.75.refs_0_.flux_ref, bf16[5248,128]{1,0:T(8,128)(2,1)S(1)} %get-tuple-element.78.refs_1_, bf16[5248,128]{1,0:T(8,128)(2,1)S(1)} %get-tuple-element.79.refs_2_, s32[272,128]{1,0:T(8,128)S(1)} %get-tuple-element.80.refs_3_.refs_4_.refs_5_.tab0_ref.tab1_ref, ...), custom_call_target="tpu_custom_call" | custom-call | flops 1006632960 | bytes 20971520 | tf_op jit(solution)/shard_map/predict/pallas_call | solution.py:435
  50.2 0.0 copy-start.1
  50.2 0.0 copy-start.2
  50.3 0.0 copy-start.3
  50.3 9.1 %collective-permute-done.7.tab_ref.refs_2_.refs_3_.meta_ref = s32[272,128]{1,0:T(8,128)S(1)} collective-permute-done((s32[272,128]{1,0:T(8,128)S(1)}, s32[272,128]{1,0:T(8,128)S(1)}, u32[]{:S(2)}, u32[]{:S(2)}) %collective-permute-start.7) | collective-permute-done | bytes 139296 | tf_op jit(solution)/shard_map/ppermute | solution.py:58
  59.4 0.0 collective-permute-done.8.refs_1_
  59.4 6.7 %predict.3.other_ref = f32[8,128]{1,0:T(8,128)S(1)} custom-call(bf16[240,8192]{1,0:T(8,128)(2,1)S(1)} %get-tuple-element.75.refs_0_.flux_ref, bf16[5248,128]{1,0:T(8,128)(2,1)S(1)} %collective-permute-done.8.refs_1_, s32[272,128]{1,0:T(8,128)S(1)} %collective-permute-done.7.tab_ref.refs_2_.refs_3_.meta_ref, ...), custom_call_target="tpu_custom_call" | custom-call | flops 503316480 | bytes 15728640 | tf_op jit(solution)/shard_map/predict/pallas_call | solution.py:435
  66.0 0.0 collective-permute-done.6.rows_ref
  66.0 0.9 align.1.rows_ref
  67.0 0.0 copy-done.4
  67.0 0.0 copy-done.5
  67.0 19.9 %exchange.1 = (f32[2,8,128]{2,1,0:T(8,128)S(1)}, f32[8,128]{1,0:T(8,128)S(1)}) custom-call(bf16[240,8192]{1,0:T(8,128)(2,1)S(1)} %get-tuple-element.75.refs_0_.flux_ref, bf16[8192,128]{1,0:T(8,128)(2,1)S(1)} %align.1.rows_ref, s32[272,128]{1,0:T(8,128)S(1)} %collective-permute-done.7.tab_ref.refs_2_.refs_3_.meta_ref, f32[8,128]{1,0:T(8,128)S(1)} %predict.2.mine_ref, ...), custom_call_target="tpu_custom_call" | custom-call | flops 503316480 | bytes 31457280 | tf_op jit(solution)/shard_map/exchange/pallas_call | solution.py:611
  86.9 0.5 slice.21
  88.1 0.0 copy-done.1
  88.1 0.0 copy-done.2
  88.1 0.0 copy-done.3
  88.1 34.3 %conditional.1 = (f32[240,8192]{1,0:T(8,128)}) conditional(s32[]{:T(128)} %bitcast.11, (f32[2,8,128]{2,1,0:T(8,128)S(1)}, f32[240,8192]{1,0:T(8,128)S(1)}, bf16[5248,128]{1,0:T(8,128)(2,1)S(1)}, bf16[5248,128]{1,0:T(8,128)(2,1)S(1)}, bf16[5248,128]{1,0:T(8,128)(2,1)S(1)}, /*index=5*/bf16[5248,128]{1,0:T(8,128)(2,1)S(1)}, s32[272,128]{1,0:T(8,128)S(1)}, ...), branch_computations={%region_0.0_spmd, %region_1.4_spmd} | conditional | flops 6836399616 | bytes 253735552 | solution.py:833
  88.1 0.0 copy-start
  88.1 5.9 %edges.1 = (f32[24,8192]{1,0:T(8,128)S(1)}, f32[24,8192]{1,0:T(8,128)S(1)}) custom-call(f32[2,8,128]{2,1,0:T(8,128)S(1)} %get-tuple-element.42.w_ref, f32[240,8192]{1,0:T(8,128)S(1)} %get-tuple-element.43.ps_ref, bf16[5248,128]{1,0:T(8,128)(2,1)S(1)} %get-tuple-element.44.refs_0_, bf16[5248,128]{1,0:T(8,128)(2,1)S(1)} %get-tuple-element.45.refs_1_, ...), custom_call_target="tpu_custom_call" | custom-call | flops 100000000 | bytes 8388608 | tf_op jit(solution)/shard_map/cond/branch_0_fun/edges/pallas_call | solution.py:672
  94.0 2.3 %collective-permute-start.1 = (f32[24,8192]{1,0:T(8,128)S(1)}, f32[24,8192]{1,0:T(8,128)S(1)}, u32[]{:S(2)}, u32[]{:S(2)}) collective-permute-start(f32[24,8192]{1,0:T(8,128)S(1)} %get-tuple-element.50.head_ref), channel_id=1, source_target_pairs={{8,0},{16,8},{24,16},{32,24},{40,32},{48,40},{56,48},{64,56},{72,6... | collective-permute-start | bytes 2359304 | tf_op jit(solution)/shard_map/cond/branch_0_fun/ppermute | solution.py:58
  96.3 4.8 %collective-permute-start = (f32[24,8192]{1,0:T(8,128)S(1)}, f32[24,8192]{1,0:T(8,128)S(1)}, u32[]{:S(2)}, u32[]{:S(2)}) collective-permute-start(f32[24,8192]{1,0:T(8,128)S(1)} %get-tuple-element.51.tail_ref), channel_id=1, source_target_pairs={{0,8},{8,16},{16,24},{24,32},{32,40},{40,48},{48,56},{56,64},{64,7... | collective-permute-start | bytes 2359304 | tf_op jit(solution)/shard_map/cond/branch_0_fun/ppermute | solution.py:58
  101.1 0.0 copy-done
  101.1 17.9 %inner.1.own_ref = f32[240,8192]{1,0:T(8,128)} custom-call(f32[2,8,128]{2,1,0:T(8,128)S(1)} %get-tuple-element.42.w_ref, f32[24,8192]{1,0:T(8,128)S(1)} %get-tuple-element.50.head_ref, f32[24,8192]{1,0:T(8,128)S(1)} %get-tuple-element.51.tail_ref, bf16[240,768]{1,0:T(8,128)(2,1)S(1)} %copy-done, f32[240,8192]{1,0:T(8,128)S(1)} %get-tuple-element.43.ps_ref, ...), custom_call_target="tpu_custom_call" | custom-call | flops 4000000000 | bytes 41943040 | tf_op jit(solution)/shard_map/cond/branch_0_fun/inner/pallas_call | solution.py:736
  119.0 0.0 collective-permute-done.1.below_ref
  119.0 0.0 collective-permute-done.above_ref
  119.0 3.1 %finish.1 = f32[240,8192]{1,0:T(8,128)} custom-call(f32[240,8192]{1,0:T(8,128)} %inner.1.own_ref, f32[240,8192]{1,0:T(8,128)S(1)} %get-tuple-element.43.ps_ref, f32[24,8192]{1,0:T(8,128)S(1)} %collective-permute-done.above_ref, f32[24,8192]{1,0:T(8,128)S(1)} %collective-permute-done.1.below_ref), custom_call_target="tpu_custom_call", output_to_operand_aliasing={{}: (0, {})} | custom-call | tf_op jit(solution)/shard_map/cond/branch_0_fun/finish/pallas_call | solution.py:787
Async XLA Ops:
  16.9 42.5 %collective-permute-start.8 = (bf16[5248,128]{1,0:T(8,128)(2,1)S(1)}, bf16[5248,128]{1,0:T(8,128)(2,1)S(1)}, u32[]{:S(2)}, u32[]{:S(2)}) collective-permute-start(bf16[5248,128]{1,0:T(8,128)(2,1)S(1)} %get-tuple-element.81), channel_id=1, source_target_pairs={{8,0},{16,8},{24,16},{32,24},{40,32},{48,40},{56,48},{64,56},{72,6... | collective-permute-start | bytes 4030472 | tf_op jit(solution)/shard_map/ppermute | solution.py:58
  37.1 28.9 %collective-permute-start.6 = (bf16[5248,128]{1,0:T(8,128)(2,1)S(1)}, bf16[5248,128]{1,0:T(8,128)(2,1)S(1)}, u32[]{:S(2)}, u32[]{:S(2)}) collective-permute-start(bf16[5248,128]{1,0:T(8,128)(2,1)S(1)} %get-tuple-element.76), channel_id=1, source_target_pairs={{8,0},{16,8},{24,16},{32,24},{40,32},{48,40},{56,48},{64,56},{72,6... | collective-permute-start | bytes 4030472 | tf_op jit(solution)/shard_map/ppermute | solution.py:58
  39.0 20.3 %collective-permute-start.7 = (s32[272,128]{1,0:T(8,128)S(1)}, s32[272,128]{1,0:T(8,128)S(1)}, u32[]{:S(2)}, u32[]{:S(2)}) collective-permute-start(s32[272,128]{1,0:T(8,128)S(1)} %get-tuple-element.77), channel_id=1, source_target_pairs={{8,0},{16,8},{24,16},{32,24},{40,32},{48,40},{56,48},{64,56},{72,6... | collective-permute-start | bytes 417800 | tf_op jit(solution)/shard_map/ppermute | solution.py:58
  40.9 26.0 %copy-start.4 = (f32[1024]{0:T(1024)S(1)}, f32[1024]{0:T(1024)}, u32[]{:S(2)}) copy-start(f32[1024]{0:T(1024)} %param.14) | copy-start | bytes 12292
  40.9 26.0 %copy-start.5 = (f32[1024]{0:T(1024)S(1)}, f32[1024]{0:T(1024)}, u32[]{:S(2)}) copy-start(f32[1024]{0:T(1024)} %param.15) | copy-start | bytes 12292
  50.2 37.8 %copy-start.1 = (s32[1024,16]{0,1:T(8,128)S(1)}, s32[1024,16]{0,1:T(8,128)}, u32[]{:S(2)}) copy-start(s32[1024,16]{0,1:T(8,128)} %param.17) | copy-start | bytes 196612
  50.2 37.8 %copy-start.2 = (s32[1024,16]{0,1:T(8,128)S(1)}, s32[1024,16]{0,1:T(8,128)}, u32[]{:S(2)}) copy-start(s32[1024,16]{0,1:T(8,128)} %param.18) | copy-start | bytes 196612
  50.3 37.8 %copy-start.3 = (s32[1024]{0:T(1024)S(1)}, s32[1024]{0:T(1024)}, u32[]{:S(2)}) copy-start(s32[1024]{0:T(1024)} %param.16) | copy-start | bytes 12292
  88.1 13.0 %copy-start = (bf16[240,768]{1,0:T(8,128)(2,1)S(1)}, bf16[240,768]{1,0:T(8,128)(2,1)}, u32[]{:S(2)}) copy-start(bf16[240,768]{1,0:T(8,128)(2,1)} %constant.25.clone.1.kern_ref) | copy-start | bytes 1105924 | tf_op jit(solution)/shard_map/cond
  94.0 25.0 %collective-permute-start.1 = (f32[24,8192]{1,0:T(8,128)S(1)}, f32[24,8192]{1,0:T(8,128)S(1)}, u32[]{:S(2)}, u32[]{:S(2)}) collective-permute-start(f32[24,8192]{1,0:T(8,128)S(1)} %get-tuple-element.50.head_ref), channel_id=1, source_target_pairs={{8,0},{16,8},{24,16},{32,24},{40,32},{48,40},{56,48},{64,56},{72,6... | collective-permute-start | bytes 2359304 | tf_op jit(solution)/shard_map/cond/branch_0_fun/ppermute | solution.py:58
  96.3 22.7 %collective-permute-start = (f32[24,8192]{1,0:T(8,128)S(1)}, f32[24,8192]{1,0:T(8,128)S(1)}, u32[]{:S(2)}, u32[]{:S(2)}) collective-permute-start(f32[24,8192]{1,0:T(8,128)S(1)} %get-tuple-element.51.tail_ref), channel_id=1, source_target_pairs={{0,8},{8,16},{16,24},{24,32},{32,40},{40,48},{48,56},{56,64},{64,7... | collective-permute-start | bytes 2359304 | tf_op jit(solution)/shard_map/cond/branch_0_fun/ppermute | solution.py:58

commit v2 on v1

--- a/solution.py
+++ b/solution.py
@@ -395,7 +395,7 @@
     return lines
 
 
-def predict_binned(flux_ref, rows_ref, meta_ref, first):
+def predict_binned(flux_ref, rows_ref, meta_ref, first, begin, end, acc):
     hours = iota((flux_ref.shape[0], LANES), 0) + 1
     eight, bins = iota((8, LANES), 0), iota((LANES, LANES), 0)
     step = 8
@@ -417,8 +417,7 @@
                                         jnp.concatenate(right[at:at + 2], axis=1), NT, preferred_element_type=F32)
         return acc
 
-    acc = lax.fori_loop(0, CELLS // step, group, jnp.zeros((16, LANES), F32))
-    return acc[:4] + acc[8:12]
+    return lax.fori_loop(begin // step, end // step, group, acc)
 
 
 def predict_body(k, *refs):
@@ -475,9 +474,8 @@
             greet((w + 1, peers[d]))
 
     flag0[...] = jnp.maximum(tab0_ref[...], tab1_ref[...]).astype(F32)
-    lines = predict_binned(flux_ref, rows_ref, meta_ref, META)
-    later = jnp.concatenate([jnp.zeros((4, LANES), F32), lines], axis=0) + other_ref[...]
-    later_ref[...] = later
+    pause = 40
+    acc = predict_binned(flux_ref, rows_ref, meta_ref, META, 0, pause, jnp.zeros((16, LANES), F32))
     sides = jnp.where(up, 1, 0) + jnp.where(down, 1, 0)
     pl.semaphore_wait(barrier, tiles - 1 + wins - 1 + sides * (tiles - 1))
 
@@ -514,6 +512,9 @@
         for copy in obs_to(w - 1):
             copy.start()
 
+    acc = predict_binned(flux_ref, rows_ref, meta_ref, META, pause, CELLS, acc)
+    later = jnp.concatenate([jnp.zeros((4, LANES), F32), acc[:4] + acc[8:12]], axis=0) + other_ref[...]
+    later_ref[...] = later
     for d in range(1, tiles):
         peer(1, d, t).start()
 
@@ -647,8 +648,8 @@
     tables = [w_ref[0], w_ref[1]]
 
     def group(g, _):
-        for u in range(4):
-            b = g * 4 + u
+        for u in range(8):
+            b = g * 8 + u
             codes = [metas[i // 2][pl.ds((i % 2) * META + b, 1), :] for i in range(4)]
             code = codes[0]
             fps = []
@@ -664,7 +665,7 @@
             tail_ref[:, col] = part[KH:] * ps_ref[total - KH:, col]
         return 0
 
-    lax.fori_loop(0, CELLS // 4, group, 0)
+    lax.fori_loop(0, CELLS // 8, group, 0)
 
 
 def edges(w, ps, rows, metas):

time: 123 us -> 119 us (0.967)
  Pallas kernels: 97.4 us -> 93.5 us
    pallas_call x1, Pallas kernels: 5.89 us -> 3.83 us  [edges(): pl.pallas_call(edges_body, grid=(1,), out_shape=(jax.ShapeDtypeStruct((KH...]
    pallas_call x1, Pallas kernels: 19.9 us -> 18.1 us  [exchange(): pl.pallas_call(exchange_body, grid=(1,), out_shape=(jax.ShapeDtypeStruct(...]
  transfers between devices with their start and end apart: 5 -> 5, of which waited for: 1 -> 1; matrix products, arithmetic and copies ran while one was open for 0% -> 0% of each run, Pallas kernels for 41% -> 43%
where the time goes in v2:
time: 119 us
  Pallas kernels  93.5 us (79%)
  starting transfers between devices  14.2 us (12%)
  waiting for transfers between devices  9.1 us (8%)
    pallas_call x2, Pallas kernels, sort_half(): pl.pallas_call(functools.partial(sort_body, nobs, which, hb), out_shape=(...  33.8 us
    pallas_call x1, Pallas kernels, exchange(): pl.pallas_call(exchange_body, grid=(1,), out_shape=(jax.ShapeDtypeStruct(...  18.1 us
    pallas_call x1, Pallas kernels, inner(): pl.pallas_call(inner_body, grid=(1,), out_shape=jax.ShapeDtypeStruct(ps.s...  17.8 us
    pallas_call x2, Pallas kernels, predict(): pl.pallas_call(functools.partial(predict_body, k), grid=(1,), out_shape=j...  15.9 us
    ppermute x5, starting transfers between devices, from_behind(): lax.ppermute(value, axis, [(source, source + steps) for source in range(i...  14.2 us
    ppermute x5, waiting for transfers between devices, from_behind(): lax.ppermute(value, axis, [(source, source + steps) for source in range(i...  9.1 us
    pallas_call x1, Pallas kernels, edges(): pl.pallas_call(edges_body, grid=(1,), out_shape=(jax.ShapeDtypeStruct((KH...  3.83 us
    pallas_call x1, Pallas kernels, finish(): pl.pallas_call(finish_body, out_shape=jax.ShapeDtypeStruct(ps.shape, F32)...  3.14 us
  transfers between devices with their start and end apart: 5, of which 1 were waited for; matrix products, arithmetic and copies ran while one was open for 0% of the time, Pallas kernels for 43%

profile of v2, /device:TPU:1, one launch (start us, length us, event | category | flops | bytes accessed | tf_op | source)
XLA Modules:
  0.0 118.7 jit_solution(653556921642281457)
XLA Ops:
  0.0 16.9 %sort_half.2 = (bf16[5248,128]{1,0:T(8,128)(2,1)S(1)}, bf16[5248,128]{1,0:T(8,128)(2,1)S(1)}, s32[136,128]{1,0:T(8,128)S(1)}, s32[136,128]{1,0:T(8,128)S(1)}) custom-call(s32[1,1024]{1,0:T(1,128)} %bitcast.21, s32[16,1024]{1,0:T(8,128)} %bitcast.17, s32[16,1024]{1,0:T(8,128)} %bitcast.19, bf16[16384,128]{1,0:T(8,128)(2,1)} %bitcast.13), custom_call_target="tpu_custom_call" | custom-call | flops 1000000000 | bytes 52428800 | tf_op jit(solution)/shard_map/sort_half/pallas_call | solution.py:340
  16.9 3.3 %collective-permute-start.8 = (bf16[5248,128]{1,0:T(8,128)(2,1)S(1)}, bf16[5248,128]{1,0:T(8,128)(2,1)S(1)}, u32[]{:S(2)}, u32[]{:S(2)}) collective-permute-start(bf16[5248,128]{1,0:T(8,128)(2,1)S(1)} %get-tuple-element.81), channel_id=1, source_target_pairs={{8,0},{16,8},{24,16},{32,24},{40,32},{48,40},{56,48},{64,56},{72,6... | collective-permute-start | bytes 4030472 | tf_op jit(solution)/shard_map/ppermute | solution.py:58
  20.2 16.9 %sort_half.3 = (bf16[5248,128]{1,0:T(8,128)(2,1)S(1)}, bf16[5248,128]{1,0:T(8,128)(2,1)S(1)}, s32[272,128]{1,0:T(8,128)S(1)}, s32[272,128]{1,0:T(8,128)S(1)}, f3...) custom-call(s32[1,1024]{1,0:T(1,128)} %bitcast.22, s32[16,1024]{1,0:T(8,128)} %bitcast.18, s32[16,1024]{1,0:T(8,128)} %bitcast.20, ...), custom_call_target="tpu_custom_call" | custom-call | flops 1000000000 | bytes 52428800 | tf_op jit(solution)/shard_map/sort_half/pallas_call | solution.py:340
  37.1 1.9 %collective-permute-start.6 = (bf16[5248,128]{1,0:T(8,128)(2,1)S(1)}, bf16[5248,128]{1,0:T(8,128)(2,1)S(1)}, u32[]{:S(2)}, u32[]{:S(2)}) collective-permute-start(bf16[5248,128]{1,0:T(8,128)(2,1)S(1)} %get-tuple-element.76), channel_id=1, source_target_pairs={{8,0},{16,8},{24,16},{32,24},{40,32},{48,40},{56,48},{64,56},{72,6... | collective-permute-start | bytes 4030472 | tf_op jit(solution)/shard_map/ppermute | solution.py:58
  39.0 1.9 %collective-permute-start.7 = (s32[272,128]{1,0:T(8,128)S(1)}, s32[272,128]{1,0:T(8,128)S(1)}, u32[]{:S(2)}, u32[]{:S(2)}) collective-permute-start(s32[272,128]{1,0:T(8,128)S(1)} %get-tuple-element.77), channel_id=1, source_target_pairs={{8,0},{16,8},{24,16},{32,24},{40,32},{48,40},{56,48},{64,56},{72,6... | collective-permute-start | bytes 417800 | tf_op jit(solution)/shard_map/ppermute | solution.py:58
  40.9 0.0 copy-start.4
  40.9 0.0 copy-start.5
  41.0 9.3 %predict.2.mine_ref = f32[8,128]{1,0:T(8,128)S(1)} custom-call(bf16[240,8192]{1,0:T(8,128)(2,1)S(1)} %get-tuple-element.75.refs_0_.flux_ref, bf16[5248,128]{1,0:T(8,128)(2,1)S(1)} %get-tuple-element.78.refs_1_, bf16[5248,128]{1,0:T(8,128)(2,1)S(1)} %get-tuple-element.79.refs_2_, s32[272,128]{1,0:T(8,128)S(1)} %get-tuple-element.80.refs_3_.refs_4_.refs_5_.tab0_ref.tab1_ref, ...), custom_call_target="tpu_custom_call" | custom-call | flops 1006632960 | bytes 20971520 | tf_op jit(solution)/shard_map/predict/pallas_call | solution.py:434
  50.2 0.0 copy-start.1
  50.2 0.0 copy-start.2
  50.3 0.0 copy-start.3
  50.3 9.1 %collective-permute-done.7.tab_ref.refs_2_.refs_3_.meta_ref = s32[272,128]{1,0:T(8,128)S(1)} collective-permute-done((s32[272,128]{1,0:T(8,128)S(1)}, s32[272,128]{1,0:T(8,128)S(1)}, u32[]{:S(2)}, u32[]{:S(2)}) %collective-permute-start.7) | collective-permute-done | bytes 139296 | tf_op jit(solution)/shard_map/ppermute | solution.py:58
  59.4 0.0 collective-permute-done.8.refs_1_
  59.4 6.7 %predict.3.other_ref = f32[8,128]{1,0:T(8,128)S(1)} custom-call(bf16[240,8192]{1,0:T(8,128)(2,1)S(1)} %get-tuple-element.75.refs_0_.flux_ref, bf16[5248,128]{1,0:T(8,128)(2,1)S(1)} %collective-permute-done.8.refs_1_, s32[272,128]{1,0:T(8,128)S(1)} %collective-permute-done.7.tab_ref.refs_2_.refs_3_.meta_ref, ...), custom_call_target="tpu_custom_call" | custom-call | flops 503316480 | bytes 15728640 | tf_op jit(solution)/shard_map/predict/pallas_call | solution.py:434
  66.0 0.0 collective-permute-done.6.rows_ref
  66.0 0.9 align.1.rows_ref
  67.0 0.0 copy-done.4
  67.0 0.0 copy-done.5
  67.0 18.1 %exchange.1 = (f32[2,8,128]{2,1,0:T(8,128)S(1)}, f32[8,128]{1,0:T(8,128)S(1)}) custom-call(bf16[240,8192]{1,0:T(8,128)(2,1)S(1)} %get-tuple-element.75.refs_0_.flux_ref, bf16[8192,128]{1,0:T(8,128)(2,1)S(1)} %align.1.rows_ref, s32[272,128]{1,0:T(8,128)S(1)} %collective-permute-done.7.tab_ref.refs_2_.refs_3_.meta_ref, f32[8,128]{1,0:T(8,128)S(1)} %predict.2.mine_ref, ...), custom_call_target="tpu_custom_call" | custom-call | flops 503316480 | bytes 31457280 | tf_op jit(solution)/shard_map/exchange/pallas_call | solution.py:612
  85.1 0.5 slice.21
  86.2 0.0 copy-done.1
  86.3 0.0 copy-done.2
  86.3 0.0 copy-done.3
  86.3 32.2 %conditional.1 = (f32[240,8192]{1,0:T(8,128)}) conditional(s32[]{:T(128)} %bitcast.11, (f32[2,8,128]{2,1,0:T(8,128)S(1)}, f32[240,8192]{1,0:T(8,128)S(1)}, bf16[5248,128]{1,0:T(8,128)(2,1)S(1)}, bf16[5248,128]{1,0:T(8,128)(2,1)S(1)}, bf16[5248,128]{1,0:T(8,128)(2,1)S(1)}, /*index=5*/bf16[5248,128]{1,0:T(8,128)(2,1)S(1)}, s32[272,128]{1,0:T(8,128)S(1)}, ...), branch_computations={%region_0.0_spmd, %region_1.4_spmd} | conditional | flops 6836399616 | bytes 253735552 | solution.py:834
  86.3 0.0 copy-start
  86.3 3.8 %edges.1 = (f32[24,8192]{1,0:T(8,128)S(1)}, f32[24,8192]{1,0:T(8,128)S(1)}) custom-call(f32[2,8,128]{2,1,0:T(8,128)S(1)} %get-tuple-element.42.w_ref, f32[240,8192]{1,0:T(8,128)S(1)} %get-tuple-element.43.ps_ref, bf16[5248,128]{1,0:T(8,128)(2,1)S(1)} %get-tuple-element.44.refs_0_, bf16[5248,128]{1,0:T(8,128)(2,1)S(1)} %get-tuple-element.45.refs_1_, ...), custom_call_target="tpu_custom_call" | custom-call | flops 100000000 | bytes 8388608 | tf_op jit(solution)/shard_map/cond/branch_0_fun/edges/pallas_call | solution.py:673
  90.1 2.3 %collective-permute-start.1 = (f32[24,8192]{1,0:T(8,128)S(1)}, f32[24,8192]{1,0:T(8,128)S(1)}, u32[]{:S(2)}, u32[]{:S(2)}) collective-permute-start(f32[24,8192]{1,0:T(8,128)S(1)} %get-tuple-element.50.head_ref), channel_id=1, source_target_pairs={{8,0},{16,8},{24,16},{32,24},{40,32},{48,40},{56,48},{64,56},{72,6... | collective-permute-start | bytes 2359304 | tf_op jit(solution)/shard_map/cond/branch_0_fun/ppermute | solution.py:58
  92.4 4.8 %collective-permute-start = (f32[24,8192]{1,0:T(8,128)S(1)}, f32[24,8192]{1,0:T(8,128)S(1)}, u32[]{:S(2)}, u32[]{:S(2)}) collective-permute-start(f32[24,8192]{1,0:T(8,128)S(1)} %get-tuple-element.51.tail_ref), channel_id=1, source_target_pairs={{0,8},{8,16},{16,24},{24,32},{32,40},{40,48},{48,56},{56,64},{64,7... | collective-permute-start | bytes 2359304 | tf_op jit(solution)/shard_map/cond/branch_0_fun/ppermute | solution.py:58
  97.2 0.0 copy-done
  97.2 17.8 %inner.1.own_ref = f32[240,8192]{1,0:T(8,128)} custom-call(f32[2,8,128]{2,1,0:T(8,128)S(1)} %get-tuple-element.42.w_ref, f32[24,8192]{1,0:T(8,128)S(1)} %get-tuple-element.50.head_ref, f32[24,8192]{1,0:T(8,128)S(1)} %get-tuple-element.51.tail_ref, bf16[240,768]{1,0:T(8,128)(2,1)S(1)} %copy-done, f32[240,8192]{1,0:T(8,128)S(1)} %get-tuple-element.43.ps_ref, ...), custom_call_target="tpu_custom_call" | custom-call | flops 4000000000 | bytes 41943040 | tf_op jit(solution)/shard_map/cond/branch_0_fun/inner/pallas_call | solution.py:737
  115.1 0.0 collective-permute-done.1.below_ref
  115.1 0.0 collective-permute-done.above_ref
  115.1 3.1 %finish.1 = f32[240,8192]{1,0:T(8,128)} custom-call(f32[240,8192]{1,0:T(8,128)} %inner.1.own_ref, f32[240,8192]{1,0:T(8,128)S(1)} %get-tuple-element.43.ps_ref, f32[24,8192]{1,0:T(8,128)S(1)} %collective-permute-done.above_ref, f32[24,8192]{1,0:T(8,128)S(1)} %collective-permute-done.1.below_ref), custom_call_target="tpu_custom_call", output_to_operand_aliasing={{}: (0, {})} | custom-call | tf_op jit(solution)/shard_map/cond/branch_0_fun/finish/pallas_call | solution.py:788
Async XLA Ops:
  16.9 42.5 %collective-permute-start.8 = (bf16[5248,128]{1,0:T(8,128)(2,1)S(1)}, bf16[5248,128]{1,0:T(8,128)(2,1)S(1)}, u32[]{:S(2)}, u32[]{:S(2)}) collective-permute-start(bf16[5248,128]{1,0:T(8,128)(2,1)S(1)} %get-tuple-element.81), channel_id=1, source_target_pairs={{8,0},{16,8},{24,16},{32,24},{40,32},{48,40},{56,48},{64,56},{72,6... | collective-permute-start | bytes 4030472 | tf_op jit(solution)/shard_map/ppermute | solution.py:58
  37.1 28.9 %collective-permute-start.6 = (bf16[5248,128]{1,0:T(8,128)(2,1)S(1)}, bf16[5248,128]{1,0:T(8,128)(2,1)S(1)}, u32[]{:S(2)}, u32[]{:S(2)}) collective-permute-start(bf16[5248,128]{1,0:T(8,128)(2,1)S(1)} %get-tuple-element.76), channel_id=1, source_target_pairs={{8,0},{16,8},{24,16},{32,24},{40,32},{48,40},{56,48},{64,56},{72,6... | collective-permute-start | bytes 4030472 | tf_op jit(solution)/shard_map/ppermute | solution.py:58
  39.0 20.3 %collective-permute-start.7 = (s32[272,128]{1,0:T(8,128)S(1)}, s32[272,128]{1,0:T(8,128)S(1)}, u32[]{:S(2)}, u32[]{:S(2)}) collective-permute-start(s32[272,128]{1,0:T(8,128)S(1)} %get-tuple-element.77), channel_id=1, source_target_pairs={{8,0},{16,8},{24,16},{32,24},{40,32},{48,40},{56,48},{64,56},{72,6... | collective-permute-start | bytes 417800 | tf_op jit(solution)/shard_map/ppermute | solution.py:58
  40.9 26.0 %copy-start.4 = (f32[1024]{0:T(1024)S(1)}, f32[1024]{0:T(1024)}, u32[]{:S(2)}) copy-start(f32[1024]{0:T(1024)} %param.14) | copy-start | bytes 12292
  40.9 26.0 %copy-start.5 = (f32[1024]{0:T(1024)S(1)}, f32[1024]{0:T(1024)}, u32[]{:S(2)}) copy-start(f32[1024]{0:T(1024)} %param.15) | copy-start | bytes 12292
  50.2 36.0 %copy-start.1 = (s32[1024,16]{0,1:T(8,128)S(1)}, s32[1024,16]{0,1:T(8,128)}, u32[]{:S(2)}) copy-start(s32[1024,16]{0,1:T(8,128)} %param.17) | copy-start | bytes 196612
  50.2 36.0 %copy-start.2 = (s32[1024,16]{0,1:T(8,128)S(1)}, s32[1024,16]{0,1:T(8,128)}, u32[]{:S(2)}) copy-start(s32[1024,16]{0,1:T(8,128)} %param.18) | copy-start | bytes 196612
  50.3 36.0 %copy-start.3 = (s32[1024]{0:T(1024)S(1)}, s32[1024]{0:T(1024)}, u32[]{:S(2)}) copy-start(s32[1024]{0:T(1024)} %param.16) | copy-start | bytes 12292
  86.3 10.9 %copy-start = (bf16[240,768]{1,0:T(8,128)(2,1)S(1)}, bf16[240,768]{1,0:T(8,128)(2,1)}, u32[]{:S(2)}) copy-start(bf16[240,768]{1,0:T(8,128)(2,1)} %constant.25.clone.1.kern_ref) | copy-start | bytes 1105924 | tf_op jit(solution)/shard_map/cond
  90.1 24.9 %collective-permute-start.1 = (f32[24,8192]{1,0:T(8,128)S(1)}, f32[24,8192]{1,0:T(8,128)S(1)}, u32[]{:S(2)}, u32[]{:S(2)}) collective-permute-start(f32[24,8192]{1,0:T(8,128)S(1)} %get-tuple-element.50.head_ref), channel_id=1, source_target_pairs={{8,0},{16,8},{24,16},{32,24},{40,32},{48,40},{56,48},{64,56},{72,6... | collective-permute-start | bytes 2359304 | tf_op jit(solution)/shard_map/cond/branch_0_fun/ppermute | solution.py:58
  92.4 22.6 %collective-permute-start = (f32[24,8192]{1,0:T(8,128)S(1)}, f32[24,8192]{1,0:T(8,128)S(1)}, u32[]{:S(2)}, u32[]{:S(2)}) collective-permute-start(f32[24,8192]{1,0:T(8,128)S(1)} %get-tuple-element.51.tail_ref), channel_id=1, source_target_pairs={{0,8},{8,16},{16,24},{24,32},{32,40},{40,48},{48,56},{56,64},{64,7... | collective-permute-start | bytes 2359304 | tf_op jit(solution)/shard_map/cond/branch_0_fun/ppermute | solution.py:58

commit v3 on v2

--- a/solution.py
+++ b/solution.py
@@ -768,8 +768,8 @@
         at = pl.ds(side * (total - KH), KH)
 
         def fill(q, _):
-            for u in range(4):
-                cut = pl.ds(pl.multiple_of((q * 4 + u) * LANES, LANES), LANES)
+            for u in range(8):
+                cut = pl.ds(pl.multiple_of((q * 8 + u) * LANES, LANES), LANES)
                 x = halo_ref[:, cut] * scale
                 for s in (1, 2, 4, 8, 16):
                     gap = jnp.zeros((s, LANES), F32)
@@ -778,7 +778,7 @@
                 ownv[side, :, cut] = ownv[side, :, cut] + ps_ref[at, cut] * (x * after)
             return 0
 
-        lax.fori_loop(0, ps_ref.shape[1] // LANES // 4, fill, 0)
+        lax.fori_loop(0, ps_ref.shape[1] // LANES // 8, fill, 0)
         store(side).start()
     for side in range(2):
         store(side).wait()

time: 119 us -> 119 us (level)
  no operation moved by 1% of the time
where the time goes in v3:
time: 119 us
  Pallas kernels  93.4 us (78%)
  starting transfers between devices  14.2 us (12%)
  waiting for transfers between devices  9.1 us (8%)
    pallas_call x2, Pallas kernels, sort_half(): pl.pallas_call(functools.partial(sort_body, nobs, which, hb), out_shape=(...  33.8 us
    pallas_call x1, Pallas kernels, exchange(): pl.pallas_call(exchange_body, grid=(1,), out_shape=(jax.ShapeDtypeStruct(...  18.1 us
    pallas_call x1, Pallas kernels, inner(): pl.pallas_call(inner_body, grid=(1,), out_shape=jax.ShapeDtypeStruct(ps.s...  17.8 us
    pallas_call x2, Pallas kernels, predict(): pl.pallas_call(functools.partial(predict_body, k), grid=(1,), out_shape=j...  15.9 us
    ppermute x5, starting transfers between devices, from_behind(): lax.ppermute(value, axis, [(source, source + steps) for source in range(i...  14.2 us
    ppermute x5, waiting for transfers between devices, from_behind(): lax.ppermute(value, axis, [(source, source + steps) for source in range(i...  9.1 us
    pallas_call x1, Pallas kernels, edges(): pl.pallas_call(edges_body, grid=(1,), out_shape=(jax.ShapeDtypeStruct((KH...  3.83 us
    pallas_call x1, Pallas kernels, finish(): pl.pallas_call(finish_body, out_shape=jax.ShapeDtypeStruct(ps.shape, F32)...  2.99 us
  transfers between devices with their start and end apart: 5, of which 1 were waited for; matrix products, arithmetic and copies ran while one was open for 0% of the time, Pallas kernels for 43%

profile of v3, /device:TPU:1, one launch (start us, length us, event | category | flops | bytes accessed | tf_op | source)
XLA Modules:
  0.0 118.6 jit_solution(10300472635790027351)
XLA Ops:
  0.0 16.9 %sort_half.2 = (bf16[5248,128]{1,0:T(8,128)(2,1)S(1)}, bf16[5248,128]{1,0:T(8,128)(2,1)S(1)}, s32[136,128]{1,0:T(8,128)S(1)}, s32[136,128]{1,0:T(8,128)S(1)}) custom-call(s32[1,1024]{1,0:T(1,128)} %bitcast.21, s32[16,1024]{1,0:T(8,128)} %bitcast.17, s32[16,1024]{1,0:T(8,128)} %bitcast.19, bf16[16384,128]{1,0:T(8,128)(2,1)} %bitcast.13), custom_call_target="tpu_custom_call" | custom-call | flops 1000000000 | bytes 52428800 | tf_op jit(solution)/shard_map/sort_half/pallas_call | solution.py:340
  16.9 3.3 %collective-permute-start.8 = (bf16[5248,128]{1,0:T(8,128)(2,1)S(1)}, bf16[5248,128]{1,0:T(8,128)(2,1)S(1)}, u32[]{:S(2)}, u32[]{:S(2)}) collective-permute-start(bf16[5248,128]{1,0:T(8,128)(2,1)S(1)} %get-tuple-element.81), channel_id=1, source_target_pairs={{8,0},{16,8},{24,16},{32,24},{40,32},{48,40},{56,48},{64,56},{72,6... | collective-permute-start | bytes 4030472 | tf_op jit(solution)/shard_map/ppermute | solution.py:58
  20.2 16.9 %sort_half.3 = (bf16[5248,128]{1,0:T(8,128)(2,1)S(1)}, bf16[5248,128]{1,0:T(8,128)(2,1)S(1)}, s32[272,128]{1,0:T(8,128)S(1)}, s32[272,128]{1,0:T(8,128)S(1)}, f3...) custom-call(s32[1,1024]{1,0:T(1,128)} %bitcast.22, s32[16,1024]{1,0:T(8,128)} %bitcast.18, s32[16,1024]{1,0:T(8,128)} %bitcast.20, ...), custom_call_target="tpu_custom_call" | custom-call | flops 1000000000 | bytes 52428800 | tf_op jit(solution)/shard_map/sort_half/pallas_call | solution.py:340
  37.1 1.9 %collective-permute-start.6 = (bf16[5248,128]{1,0:T(8,128)(2,1)S(1)}, bf16[5248,128]{1,0:T(8,128)(2,1)S(1)}, u32[]{:S(2)}, u32[]{:S(2)}) collective-permute-start(bf16[5248,128]{1,0:T(8,128)(2,1)S(1)} %get-tuple-element.76), channel_id=1, source_target_pairs={{8,0},{16,8},{24,16},{32,24},{40,32},{48,40},{56,48},{64,56},{72,6... | collective-permute-start | bytes 4030472 | tf_op jit(solution)/shard_map/ppermute | solution.py:58
  39.0 1.9 %collective-permute-start.7 = (s32[272,128]{1,0:T(8,128)S(1)}, s32[272,128]{1,0:T(8,128)S(1)}, u32[]{:S(2)}, u32[]{:S(2)}) collective-permute-start(s32[272,128]{1,0:T(8,128)S(1)} %get-tuple-element.77), channel_id=1, source_target_pairs={{8,0},{16,8},{24,16},{32,24},{40,32},{48,40},{56,48},{64,56},{72,6... | collective-permute-start | bytes 417800 | tf_op jit(solution)/shard_map/ppermute | solution.py:58
  40.9 0.0 copy-start.4
  40.9 0.0 copy-start.5
  41.0 9.3 %predict.2.mine_ref = f32[8,128]{1,0:T(8,128)S(1)} custom-call(bf16[240,8192]{1,0:T(8,128)(2,1)S(1)} %get-tuple-element.75.refs_0_.flux_ref, bf16[5248,128]{1,0:T(8,128)(2,1)S(1)} %get-tuple-element.78.refs_1_, bf16[5248,128]{1,0:T(8,128)(2,1)S(1)} %get-tuple-element.79.refs_2_, s32[272,128]{1,0:T(8,128)S(1)} %get-tuple-element.80.refs_3_.refs_4_.refs_5_.tab0_ref.tab1_ref, ...), custom_call_target="tpu_custom_call" | custom-call | flops 1006632960 | bytes 20971520 | tf_op jit(solution)/shard_map/predict/pallas_call | solution.py:434
  50.2 0.0 copy-start.1
  50.2 0.0 copy-start.2
  50.3 0.0 copy-start.3
  50.3 9.1 %collective-permute-done.7.tab_ref.refs_2_.refs_3_.meta_ref = s32[272,128]{1,0:T(8,128)S(1)} collective-permute-done((s32[272,128]{1,0:T(8,128)S(1)}, s32[272,128]{1,0:T(8,128)S(1)}, u32[]{:S(2)}, u32[]{:S(2)}) %collective-permute-start.7) | collective-permute-done | bytes 139296 | tf_op jit(solution)/shard_map/ppermute | solution.py:58
  59.4 0.0 collective-permute-done.8.refs_1_
  59.4 6.7 %predict.3.other_ref = f32[8,128]{1,0:T(8,128)S(1)} custom-call(bf16[240,8192]{1,0:T(8,128)(2,1)S(1)} %get-tuple-element.75.refs_0_.flux_ref, bf16[5248,128]{1,0:T(8,128)(2,1)S(1)} %collective-permute-done.8.refs_1_, s32[272,128]{1,0:T(8,128)S(1)} %collective-permute-done.7.tab_ref.refs_2_.refs_3_.meta_ref, ...), custom_call_target="tpu_custom_call" | custom-call | flops 503316480 | bytes 15728640 | tf_op jit(solution)/shard_map/predict/pallas_call | solution.py:434
  66.0 0.0 collective-permute-done.6.rows_ref
  66.0 0.9 align.1.rows_ref
  67.0 0.0 copy-done.4
  67.0 0.0 copy-done.5
  67.0 18.1 %exchange.1 = (f32[2,8,128]{2,1,0:T(8,128)S(1)}, f32[8,128]{1,0:T(8,128)S(1)}) custom-call(bf16[240,8192]{1,0:T(8,128)(2,1)S(1)} %get-tuple-element.75.refs_0_.flux_ref, bf16[8192,128]{1,0:T(8,128)(2,1)S(1)} %align.1.rows_ref, s32[272,128]{1,0:T(8,128)S(1)} %collective-permute-done.7.tab_ref.refs_2_.refs_3_.meta_ref, f32[8,128]{1,0:T(8,128)S(1)} %predict.2.mine_ref, ...), custom_call_target="tpu_custom_call" | custom-call | flops 503316480 | bytes 31457280 | tf_op jit(solution)/shard_map/exchange/pallas_call | solution.py:612
  85.1 0.5 slice.21
  86.2 0.0 copy-done.1
  86.3 0.0 copy-done.2
  86.3 0.0 copy-done.3
  86.3 32.1 %conditional.1 = (f32[240,8192]{1,0:T(8,128)}) conditional(s32[]{:T(128)} %bitcast.11, (f32[2,8,128]{2,1,0:T(8,128)S(1)}, f32[240,8192]{1,0:T(8,128)S(1)}, bf16[5248,128]{1,0:T(8,128)(2,1)S(1)}, bf16[5248,128]{1,0:T(8,128)(2,1)S(1)}, bf16[5248,128]{1,0:T(8,128)(2,1)S(1)}, /*index=5*/bf16[5248,128]{1,0:T(8,128)(2,1)S(1)}, s32[272,128]{1,0:T(8,128)S(1)}, ...), branch_computations={%region_0.0_spmd, %region_1.4_spmd} | conditional | flops 6836399616 | bytes 253735552 | solution.py:834
  86.3 0.0 copy-start
  86.3 3.8 %edges.1 = (f32[24,8192]{1,0:T(8,128)S(1)}, f32[24,8192]{1,0:T(8,128)S(1)}) custom-call(f32[2,8,128]{2,1,0:T(8,128)S(1)} %get-tuple-element.42.w_ref, f32[240,8192]{1,0:T(8,128)S(1)} %get-tuple-element.43.ps_ref, bf16[5248,128]{1,0:T(8,128)(2,1)S(1)} %get-tuple-element.44.refs_0_, bf16[5248,128]{1,0:T(8,128)(2,1)S(1)} %get-tuple-element.45.refs_1_, ...), custom_call_target="tpu_custom_call" | custom-call | flops 100000000 | bytes 8388608 | tf_op jit(solution)/shard_map/cond/branch_0_fun/edges/pallas_call | solution.py:673
  90.1 2.3 %collective-permute-start.1 = (f32[24,8192]{1,0:T(8,128)S(1)}, f32[24,8192]{1,0:T(8,128)S(1)}, u32[]{:S(2)}, u32[]{:S(2)}) collective-permute-start(f32[24,8192]{1,0:T(8,128)S(1)} %get-tuple-element.50.head_ref), channel_id=1, source_target_pairs={{8,0},{16,8},{24,16},{32,24},{40,32},{48,40},{56,48},{64,56},{72,6... | collective-permute-start | bytes 2359304 | tf_op jit(solution)/shard_map/cond/branch_0_fun/ppermute | solution.py:58
  92.4 4.8 %collective-permute-start = (f32[24,8192]{1,0:T(8,128)S(1)}, f32[24,8192]{1,0:T(8,128)S(1)}, u32[]{:S(2)}, u32[]{:S(2)}) collective-permute-start(f32[24,8192]{1,0:T(8,128)S(1)} %get-tuple-element.51.tail_ref), channel_id=1, source_target_pairs={{0,8},{8,16},{16,24},{24,32},{32,40},{40,48},{48,56},{56,64},{64,7... | collective-permute-start | bytes 2359304 | tf_op jit(solution)/shard_map/cond/branch_0_fun/ppermute | solution.py:58
  97.2 0.0 copy-done
  97.2 17.8 %inner.1.own_ref = f32[240,8192]{1,0:T(8,128)} custom-call(f32[2,8,128]{2,1,0:T(8,128)S(1)} %get-tuple-element.42.w_ref, f32[24,8192]{1,0:T(8,128)S(1)} %get-tuple-element.50.head_ref, f32[24,8192]{1,0:T(8,128)S(1)} %get-tuple-element.51.tail_ref, bf16[240,768]{1,0:T(8,128)(2,1)S(1)} %copy-done, f32[240,8192]{1,0:T(8,128)S(1)} %get-tuple-element.43.ps_ref, ...), custom_call_target="tpu_custom_call" | custom-call | flops 4000000000 | bytes 41943040 | tf_op jit(solution)/shard_map/cond/branch_0_fun/inner/pallas_call | solution.py:737
  115.1 0.0 collective-permute-done.1.below_ref
  115.1 0.0 collective-permute-done.above_ref
  115.1 3.0 %finish.1 = f32[240,8192]{1,0:T(8,128)} custom-call(f32[240,8192]{1,0:T(8,128)} %inner.1.own_ref, f32[240,8192]{1,0:T(8,128)S(1)} %get-tuple-element.43.ps_ref, f32[24,8192]{1,0:T(8,128)S(1)} %collective-permute-done.above_ref, f32[24,8192]{1,0:T(8,128)S(1)} %collective-permute-done.1.below_ref), custom_call_target="tpu_custom_call", output_to_operand_aliasing={{}: (0, {})} | custom-call | tf_op jit(solution)/shard_map/cond/branch_0_fun/finish/pallas_call | solution.py:788
Async XLA Ops:
  16.9 42.5 %collective-permute-start.8 = (bf16[5248,128]{1,0:T(8,128)(2,1)S(1)}, bf16[5248,128]{1,0:T(8,128)(2,1)S(1)}, u32[]{:S(2)}, u32[]{:S(2)}) collective-permute-start(bf16[5248,128]{1,0:T(8,128)(2,1)S(1)} %get-tuple-element.81), channel_id=1, source_target_pairs={{8,0},{16,8},{24,16},{32,24},{40,32},{48,40},{56,48},{64,56},{72,6... | collective-permute-start | bytes 4030472 | tf_op jit(solution)/shard_map/ppermute | solution.py:58
  37.1 28.9 %collective-permute-start.6 = (bf16[5248,128]{1,0:T(8,128)(2,1)S(1)}, bf16[5248,128]{1,0:T(8,128)(2,1)S(1)}, u32[]{:S(2)}, u32[]{:S(2)}) collective-permute-start(bf16[5248,128]{1,0:T(8,128)(2,1)S(1)} %get-tuple-element.76), channel_id=1, source_target_pairs={{8,0},{16,8},{24,16},{32,24},{40,32},{48,40},{56,48},{64,56},{72,6... | collective-permute-start | bytes 4030472 | tf_op jit(solution)/shard_map/ppermute | solution.py:58
  39.0 20.3 %collective-permute-start.7 = (s32[272,128]{1,0:T(8,128)S(1)}, s32[272,128]{1,0:T(8,128)S(1)}, u32[]{:S(2)}, u32[]{:S(2)}) collective-permute-start(s32[272,128]{1,0:T(8,128)S(1)} %get-tuple-element.77), channel_id=1, source_target_pairs={{8,0},{16,8},{24,16},{32,24},{40,32},{48,40},{56,48},{64,56},{72,6... | collective-permute-start | bytes 417800 | tf_op jit(solution)/shard_map/ppermute | solution.py:58
  40.9 26.0 %copy-start.4 = (f32[1024]{0:T(1024)S(1)}, f32[1024]{0:T(1024)}, u32[]{:S(2)}) copy-start(f32[1024]{0:T(1024)} %param.14) | copy-start | bytes 12292
  40.9 26.0 %copy-start.5 = (f32[1024]{0:T(1024)S(1)}, f32[1024]{0:T(1024)}, u32[]{:S(2)}) copy-start(f32[1024]{0:T(1024)} %param.15) | copy-start | bytes 12292
  50.2 36.0 %copy-start.1 = (s32[1024,16]{0,1:T(8,128)S(1)}, s32[1024,16]{0,1:T(8,128)}, u32[]{:S(2)}) copy-start(s32[1024,16]{0,1:T(8,128)} %param.17) | copy-start | bytes 196612
  50.2 36.0 %copy-start.2 = (s32[1024,16]{0,1:T(8,128)S(1)}, s32[1024,16]{0,1:T(8,128)}, u32[]{:S(2)}) copy-start(s32[1024,16]{0,1:T(8,128)} %param.18) | copy-start | bytes 196612
  50.3 36.0 %copy-start.3 = (s32[1024]{0:T(1024)S(1)}, s32[1024]{0:T(1024)}, u32[]{:S(2)}) copy-start(s32[1024]{0:T(1024)} %param.16) | copy-start | bytes 12292
  86.3 10.9 %copy-start = (bf16[240,768]{1,0:T(8,128)(2,1)S(1)}, bf16[240,768]{1,0:T(8,128)(2,1)}, u32[]{:S(2)}) copy-start(bf16[240,768]{1,0:T(8,128)(2,1)} %constant.25.clone.1.kern_ref) | copy-start | bytes 1105924 | tf_op jit(solution)/shard_map/cond
  90.1 24.9 %collective-permute-start.1 = (f32[24,8192]{1,0:T(8,128)S(1)}, f32[24,8192]{1,0:T(8,128)S(1)}, u32[]{:S(2)}, u32[]{:S(2)}) collective-permute-start(f32[24,8192]{1,0:T(8,128)S(1)} %get-tuple-element.50.head_ref), channel_id=1, source_target_pairs={{8,0},{16,8},{24,16},{32,24},{40,32},{48,40},{56,48},{64,56},{72,6... | collective-permute-start | bytes 2359304 | tf_op jit(solution)/shard_map/cond/branch_0_fun/ppermute | solution.py:58
  92.4 22.6 %collective-permute-start = (f32[24,8192]{1,0:T(8,128)S(1)}, f32[24,8192]{1,0:T(8,128)S(1)}, u32[]{:S(2)}, u32[]{:S(2)}) collective-permute-start(f32[24,8192]{1,0:T(8,128)S(1)} %get-tuple-element.51.tail_ref), channel_id=1, source_target_pairs={{0,8},{8,16},{16,24},{24,32},{32,40},{40,48},{48,56},{56,64},{64,7... | collective-permute-start | bytes 2359304 | tf_op jit(solution)/shard_map/cond/branch_0_fun/ppermute | solution.py:58
